TPU v7x, 32 devices: a whole 2x2x4 slice. The times are simulated.
32 devices in a mesh: wide: 16 (over z, y, x), narrow: 2 (over core).
Axes of the slice: x: 2, y: 2, z: 4, core: 2. Of those that a mesh axis runs over, the one named last changes fastest.
Arguments:
- tokens: bfloat16 [64, 1024, 576], P('wide', 'narrow'), may hold values from -6 to 6
- cotangent: bfloat16 [64, 1024, 576], P('wide', 'narrow'), may hold values from -6 to 6
- documents: int32 [64, 1024], P('wide'), may hold values from 0 to 2, as said below
- attention_master: float32 [1536, 576], P(('wide', 'narrow'))
- attention_first: float32 [1536, 576], P(('wide', 'narrow')), may hold values from -0.00036621094 to 0.00036621094
- attention_second: float32 [1536, 576], P(('wide', 'narrow')), may hold values from 2.2605614e-11 to 3.673412e-10
- feedforward_master: float32 [3, 1536, 576], P(None, ('narrow', 'wide'))
- feedforward_first: float32 [3, 1536, 576], P(None, ('narrow', 'wide')), may hold values from -0.0008544922 to 0.0008544922
- feedforward_second: float32 [3, 1536, 576], P(None, ('narrow', 'wide')), may hold values from 1.4128508e-10 to 2.2605613e-09
- gain_master: float32 [2, 576], replicated, may hold values from 0.5 to 1.5
- gain_first: float32 [2, 576], replicated, may hold values from -0.0034179688 to 0.0034179688
- gain_second: float32 [2, 576], replicated, may hold values from 2.2605613e-09 to 3.616898e-08
Outputs:
- outputs: bfloat16 [64, 1024, 576], P('wide', 'narrow')
- grad_tokens: float32 [64, 1024, 576], P('wide', 'narrow')
- grad_norm: float32 [], replicated
- attention_new: float32 [1536, 576], P(('wide', 'narrow'))
- attention_first_new: float32 [1536, 576], P(('wide', 'narrow'))
- attention_second_new: float32 [1536, 576], P(('wide', 'narrow'))
- feedforward_new: float32 [3, 1536, 576], P(None, ('narrow', 'wide'))
- feedforward_first_new: float32 [3, 1536, 576], P(None, ('narrow', 'wide'))
- feedforward_second_new: float32 [3, 1536, 576], P(None, ('narrow', 'wide'))
- gain_new: float32 [2, 576], replicated
- gain_first_new: float32 [2, 576], replicated
- gain_second_new: float32 [2, 576], replicated
Inputs may be any that keep to these rules, and one draw needn't show every extreme that they name: Each row holds three documents in order (numbers 0, 1, 2, never falling); document 1 starts at position 256 or earlier and runs through position 767 at least.
All inputs are finite; a program needn't handle non-finite values.
Results may differ from a plain program's by a relative error of at most 0.015.
Values may be sent and summed in bfloat16 or wider, within the bound.
No kernel may reach another device: no remote copies, remote signals or barrier semaphores. Data moves between devices by JAX's collectives and lax.ppermute only.
A program may use at most 192 MiB of HBM per device.

v0:
```python
import functools

import jax
import jax.numpy as jnp
import numpy as np
from jax import lax
from jax.experimental import pallas as pl
from jax.experimental.pallas import tpu as pltpu
from jax.sharding import PartitionSpec as P

D = 576
HEADS = 9
KV_HEADS = 3
RATIO = 3
HEAD_DIM = 64
HALF = 32
STEP = 10
KV_WIDTH = 192
QKV = 960
BLOCK = 256

norm_epsilon = 1e-05
adam_epsilon = 1e-08
beta_first = 0.9
beta_second = 0.999
weight_decay = 0.1
rate_matrix = 0.05
rate_gain = 0.5
clip_limit = 1.0
rotary_base = 10000.0
masked_value = -1e30

F32 = jnp.float32
BF16 = jnp.bfloat16
VMEM_LIMIT = 60 * 2**20
SHORT = pl.CostEstimate(flops=1_000_000, transcendentals=0, bytes_accessed=100_000)


def rotary_tables(length):
    frequency = np.float32(rotary_base) ** (
        np.float32(-2.0) * np.arange(HALF, dtype=np.float32) / np.float32(HEAD_DIM)
    )
    angles = np.arange(length, dtype=np.float32)[None, :] * frequency.astype(np.float32)[:, None]
    return jnp.asarray(np.cos(angles), F32), jnp.asarray(np.sin(angles), F32)


def dot(left, right, left_dim=1, right_dim=0):
    return lax.dot_general(
        left, right, (((left_dim,), (right_dim,)), ((), ())), preferred_element_type=F32
    )


def inverse_root(values):
    return lax.rsqrt(jnp.mean(values * values, axis=0, keepdims=True) + norm_epsilon)


def joined(own, other, place):
    first = place == 0
    return jnp.concatenate(
        [jnp.where(first, own, other), jnp.where(first, other, own)], axis=1
    )


def lane_sums(values):
    lanes = 128
    total = values[:, :lanes]
    for low in range(lanes, values.shape[1], lanes):
        total = total + values[:, low : low + lanes]
    return total


def norm_backward(grad_normed, normal, inverse, gain):
    scaled = grad_normed * gain
    return inverse * (scaled - normal * jnp.mean(scaled * normal, axis=0, keepdims=True))


def visible_scores(scores, start_row, place_row, low, key_low):
    inside = low >= 256 and low + BLOCK <= 768 and key_low >= 256
    if inside and key_low < low:
        return scores
    place = lax.broadcasted_iota(jnp.int32, scores.shape, 0) + key_low
    if inside:
        seen = place <= place_row
    else:
        seen = place >= start_row
        if key_low >= low:
            seen = seen & (place <= place_row)
    return jnp.where(seen, scores, masked_value)


def triple(row):
    return jnp.concatenate([row] * RATIO, axis=1)


def turn(rows, cosine, sine):
    front, behind = rows[:HALF], rows[HALF:]
    return jnp.concatenate([front * cosine - behind * sine, behind * cosine + front * sine], axis=0)


def turn_back(rows, cosine, sine):
    front, behind = rows[:HALF], rows[HALF:]
    return jnp.concatenate([front * cosine + behind * sine, behind * cosine - front * sine], axis=0)


def attention_forward_body(
    info_ref,
    own_ref,
    other_ref,
    start_ref,
    pieces_own_ref,
    pieces_other_ref,
    gain_ref,
    cosine_ref,
    sine_ref,
    residual_ref,
    query_ref,
    key_ref,
    value_ref,
    mixed_ref,
    total_ref,
    weight_ref,
    out_weight_ref,
    out_rows,
    key_rows,
    x_across,
):
    @pl.when(pl.program_id(0) == 0)
    def _():
        chunks, rows, _ = pieces_own_ref.shape
        for chunk in range(2 * chunks):
            index = info_ref[1 + chunk]
            is_own = index < chunks
            index = jnp.where(is_own, index, index - chunks)
            part = jnp.where(is_own, pieces_own_ref[index], pieces_other_ref[index])
            low = chunk * rows
            if low < QKV:
                weight_ref[low : low + rows] = part
            else:
                out_weight_ref[low - QKV : low - QKV + rows] = part
        out_rows[...] = out_weight_ref[...].T

    x = joined(own_ref[0], other_ref[0], info_ref[0])
    length = x.shape[1]
    x_across[...] = x
    x = x.astype(F32)
    normed = (x * inverse_root(x) * gain_ref[:, 0:1]).astype(BF16)
    cosine = cosine_ref[...]
    sine = sine_ref[...]
    projected = dot(weight_ref[...], normed)
    for head in range(HEADS):
        rows = slice(head * 64, head * 64 + 64)
        query_ref[0, rows] = (turn(projected[rows], cosine, sine) * HEAD_DIM ** (-0.5)).astype(
            BF16
        )
    for head in range(KV_HEADS):
        rows = slice(head * 64, head * 64 + 64)
        rotated = turn(projected[D + head * 64 : D + head * 64 + 64], cosine, sine)
        key_ref[0, rows] = rotated.astype(BF16)
        key_rows[head] = rotated.T.astype(BF16)
    value_ref[0] = projected[D + KV_WIDTH :].astype(BF16)

    def score(member, block, r):
        low, high = block * BLOCK, (block + 1) * BLOCK
        row = (member * RATIO + r) * 64
        return dot(key_rows[member, 0:high], query_ref[0, row : row + 64, low:high])

    def finish(member, block, r, scores):
        low, high = block * BLOCK, (block + 1) * BLOCK
        start_row = start_ref[0, 0:1, low:high]
        place_row = lax.broadcasted_iota(jnp.int32, (1, BLOCK), 1) + low
        scores = [
            visible_scores(scores[k : k + BLOCK], start_row, place_row, low, k)
            for k in range(0, high, BLOCK)
        ]
        top = functools.reduce(
            jnp.maximum, [jnp.max(part, axis=0, keepdims=True) for part in scores]
        )
        exponents = [jnp.exp(part - top) for part in scores]
        total = sum(jnp.sum(part, axis=0, keepdims=True) for part in exponents)
        exponent = jnp.concatenate([part.astype(BF16) for part in exponents], axis=0)
        mixed = dot(value_ref[0, member * 64 : member * 64 + 64, 0:high], exponent)
        row = (member * RATIO + r) * 64
        mixed_ref[0, row : row + 64, low:high] = (mixed * (1.0 / total)).astype(BF16)
        total_ref[0, member, r : r + 1, low:high] = top + jnp.log(total)

    items = [
        (member, block, r)
        for member in range(KV_HEADS)
        for block in range(length // BLOCK)
        for r in range(RATIO)
    ]
    ahead = [score(*item) for item in items[:2]]
    for i, item in enumerate(items):
        if i + 2 < len(items):
            ahead.append(score(*items[i + 2]))
        finish(*item, ahead.pop(0))
    residual_ref[0] = x_across[...].astype(F32) + dot(out_rows[...], mixed_ref[0])


def whole(shape):
    return pl.BlockSpec(
        tuple(shape), lambda *_: (0,) * len(shape), pipeline_mode=pl.Buffered(1)
    )


def step_spec(shape):
    return pl.BlockSpec((1,) + tuple(shape[1:]), lambda i, info: (i,) + (0,) * (len(shape) - 1))


def params():
    return pltpu.CompilerParams(dimension_semantics=("arbitrary",), vmem_limit_bytes=VMEM_LIMIT)


def attention_forward(info, own, other, start, pieces_own, pieces_other, gain, tables):
    count = other.shape[0]
    length = 2 * other.shape[2]
    outs = [
        ((count, D, length), F32),
        ((count, D, length), BF16),
        ((count, KV_WIDTH, length), BF16),
        ((count, KV_WIDTH, length), BF16),
        ((count, D, length), BF16),
        ((count, KV_HEADS, 8, length), F32),
    ]
    weights = (QKV, D), (D, D)
    return pl.pallas_call(
        attention_forward_body,
        grid_spec=pltpu.PrefetchScalarGridSpec(
            num_scalar_prefetch=1,
            grid=(count,),
            in_specs=[
                pl.BlockSpec(
                    (1,) + own.shape[1:], lambda i, info: (info[0] * count + i, 0, 0)
                ),
                step_spec(other.shape),
                step_spec(start.shape),
                whole(pieces_own.shape),
                whole(pieces_other.shape),
                whole(gain.shape),
                whole((HALF, length)),
                whole((HALF, length)),
            ],
            out_specs=[step_spec(shape) for shape, _ in outs] + [whole(shape) for shape in weights],
            scratch_shapes=[
                pltpu.VMEM((D, D), BF16),
                pltpu.VMEM((KV_HEADS, length, HEAD_DIM), BF16),
                pltpu.VMEM((D, length), BF16),
            ],
        ),
        out_shape=[jax.ShapeDtypeStruct(shape, kind) for shape, kind in outs]
        + [jax.ShapeDtypeStruct(shape, BF16) for shape in weights],
        compiler_params=params(),
        cost_estimate=pl.CostEstimate(
            flops=8_000_000_000, transcendentals=12_000_000, bytes_accessed=20_000_000
        ),
        name="attention_forward",
    )(info, own, other, start, pieces_own, pieces_other, gain, *tables)


def stacked(refs, kinds):
    parts = [ref[:, kind].reshape(-1, D) for kind in kinds for ref in refs]
    return jnp.concatenate(parts, axis=0) if len(parts) > 1 else parts[0]


def feed_body(part_count, info_ref, residual_ref, cotangent_own_ref, cotangent_other_ref, *refs):
    weight_refs = refs[:part_count], refs[part_count : 2 * part_count]
    (
        gain_ref,
        out_own_ref,
        out_other_ref,
        back_ref,
        gain_grad_ref,
        grad_own_ref,
        grad_other_ref,
        sums,
        gain_sums,
    ) = refs[2 * part_count :]
    step = pl.program_id(0)
    units = sums.shape[2] // 3
    residual = residual_ref[0]
    cotangent = jnp.where(step % 2 == 0, cotangent_own_ref[0], cotangent_other_ref[0])
    gain = gain_ref[:, 1:2]
    inverse = inverse_root(residual)
    normal = residual * inverse
    normed = (normal * gain).astype(BF16)

    @pl.when(step == 0)
    def _():
        sums[...] = jnp.zeros_like(sums)
        gain_sums[...] = jnp.zeros_like(gain_sums)

    out = residual
    grad_normed = jnp.zeros_like(residual)
    for part, parts in enumerate(weight_refs):
        pair = stacked(parts, (0, 1))
        down = stacked(parts, (2,))
        both = dot(pair, normed)
        gate, upward = both[:units], both[units:]
        grad_hidden = dot(down, cotangent)
        sigmoid_gate = jax.nn.sigmoid(gate)
        swish = gate * sigmoid_gate
        hidden = (swish * upward).astype(BF16)
        grad_gate = (
            grad_hidden * upward * (sigmoid_gate + swish * (1.0 - sigmoid_gate))
        ).astype(BF16)
        grad_upward = (grad_hidden * swish).astype(BF16)
        grads = jnp.concatenate([grad_gate, grad_upward], axis=0)
        out = out + dot(down, hidden, 0, 0)
        grad_normed = grad_normed + dot(pair, grads, 0, 0)
        sums[part, :, : 2 * units] += dot(normed, grads, 1, 1)
        sums[part, :, 2 * units :] += dot(cotangent, hidden, 1, 1)

    out = out.astype(BF16)

    @pl.when(step % 2 == 0)
    def _():
        out_own_ref[0] = out

    @pl.when(step % 2 == 1)
    def _():
        out_other_ref[0] = out

    gain_sums[...] += lane_sums(grad_normed * normal)
    back_ref[0] = (
        cotangent.astype(F32) + norm_backward(grad_normed, normal, inverse, gain)
    ).astype(BF16)

    @pl.when(step == pl.num_programs(0) - 1)
    def _():
        pieces, kinds, rows, _ = grad_own_ref.shape
        for part, grad_ref in enumerate((grad_own_ref, grad_other_ref)):
            for kind in range(kinds):
                flipped = sums[part, :, kind * units : (kind + 1) * units].astype(BF16).T
                for piece in range(pieces):
                    grad_ref[piece, kind] = flipped[piece * rows : (piece + 1) * rows]
        gain_grad_ref[...] = jnp.sum(gain_sums[...].T, axis=0, keepdims=True)


def feed_forward(info, residual, cotangent_own, cotangent_other, weights, gain, pieces):
    count, _, length = residual.shape
    half = length // 2
    part_count = len(weights) // 2
    units = sum(part.size // (3 * D) for part in weights[:part_count])
    block = (1, D, half)
    full = pl.BlockSpec(block, lambda i, info: (i // 2, 0, (i + info[0]) % 2))
    own = pl.BlockSpec(block, lambda i, info: (info[0] * count + i // 2, 0, 0))
    other = pl.BlockSpec(block, lambda i, info: (i // 2, 0, 0))
    grad_shape = (pieces, 3, units // pieces, D)
    return pl.pallas_call(
        functools.partial(feed_body, part_count),
        grid_spec=pltpu.PrefetchScalarGridSpec(
            num_scalar_prefetch=1,
            grid=(2 * count,),
            in_specs=[full, own, other]
            + [whole(weight.shape) for weight in weights]
            + [whole(gain.shape)],
            out_specs=[own, other, full, whole((1, D))] + [whole(grad_shape)] * 2,
            scratch_shapes=[
                pltpu.VMEM((2, D, 3 * units), F32),
                pltpu.VMEM((D, 128), F32),
            ],
        ),
        out_shape=[
            jax.ShapeDtypeStruct(cotangent_own.shape, BF16),
            jax.ShapeDtypeStruct(cotangent_other.shape, BF16),
            jax.ShapeDtypeStruct(residual.shape, BF16),
            jax.ShapeDtypeStruct((1, D), F32),
        ]
        + [jax.ShapeDtypeStruct(grad_shape, BF16)] * 2,
        compiler_params=params(),
        cost_estimate=pl.CostEstimate(
            flops=32_000_000_000, transcendentals=6_000_000, bytes_accessed=30_000_000
        ),
        name="feed_forward",
    )(info, residual, cotangent_own, cotangent_other, *weights, gain)


def branch_backward_body(
    grad_ref, mixed_ref, weight_ref, grad_mixed_ref, inner_ref, weight_grad_ref
):
    @pl.when(pl.program_id(0) == 0)
    def _():
        weight_grad_ref[...] = jnp.zeros_like(weight_grad_ref)

    branch = grad_ref[0]
    grad_mixed = dot(weight_ref[...], branch).astype(BF16)
    grad_mixed_ref[0] = grad_mixed
    for head in range(HEADS):
        rows = slice(head * 64, head * 64 + 64)
        inner_ref[0, head // RATIO, head % RATIO : head % RATIO + 1] = jnp.sum(
            grad_mixed[rows].astype(F32) * mixed_ref[0, rows].astype(F32), axis=0, keepdims=True
        )
    weight_grad_ref[...] += dot(mixed_ref[0], branch, 1, 1)


def branch_backward(grad, mixed, weight):
    count, _, length = grad.shape

    half = length // 2
    step = pl.BlockSpec((1, D, half), lambda i: (i // 2, 0, i % 2))
    inner = (count, KV_HEADS, 8, length)
    return pl.pallas_call(
        branch_backward_body,
        grid=(2 * count,),
        in_specs=[step, step, whole(weight.shape)],
        out_specs=[
            step,
            pl.BlockSpec((1, KV_HEADS, 8, half), lambda i: (i // 2, 0, 0, i % 2)),
            whole((D, D)),
        ],
        out_shape=[
            jax.ShapeDtypeStruct(mixed.shape, BF16),
            jax.ShapeDtypeStruct(inner, F32),
            jax.ShapeDtypeStruct((D, D), F32),
        ],
        compiler_params=params(),
        cost_estimate=SHORT,
        name="branch_backward",
    )(grad, mixed, weight)


def attention_backward_body(
    info_ref,
    own_ref,
    other_ref,
    start_ref,
    gain_ref,
    gain_row_ref,
    weight_ref,
    out_grad_ref,
    gain_second_ref,
    cosine_ref,
    sine_ref,
    query_ref,
    key_ref,
    value_ref,
    total_ref,
    grad_ref,
    inner_ref,
    projected_ref,
    kept_ref,
    sent_ref,
    key_rows,
    value_rows,
    grad_key,
    grad_value,
    weight_sums,
):
    step = pl.program_id(0)
    length = query_ref.shape[2]
    cosine = cosine_ref[...]
    sine = sine_ref[...]
    for head in range(KV_HEADS):
        rows = slice(head * 64, head * 64 + 64)
        key_rows[head] = key_ref[0, rows].T
        value_rows[head] = value_ref[0, rows].T

    def head_rows(member, r):
        return slice((member * RATIO + r) * 64, (member * RATIO + r) * 64 + 64)

    def products(member, low, key_low, r):
        keys = slice(key_low, key_low + 256)
        rows = head_rows(member, r)
        return (
            dot(key_rows[member, keys], query_ref[0, rows, low : low + BLOCK]),
            dot(value_rows[member, keys], grad_ref[0, rows, low : low + BLOCK]),
        )

    def weighted(member, low, key_low, r, scores, grad_weights):
        lanes = slice(low, low + BLOCK)
        start_row = start_ref[0, 0:1, lanes]
        place_row = lax.broadcasted_iota(jnp.int32, (1, BLOCK), 1) + low
        scores = visible_scores(scores, start_row, place_row, low, key_low)
        weights = jnp.exp(scores - total_ref[0, member, r : r + 1, lanes])
        grad_scores = weights * (grad_weights - inner_ref[0, member, r : r + 1, lanes])
        return weights.astype(BF16), grad_scores.astype(BF16)

    items = [
        (member, low, key_low, r)
        for member in range(KV_HEADS)
        for low in range(0, length, BLOCK)
        for key_low in range(0, low + BLOCK, 256)
        for r in range(RATIO)
    ]
    ahead = [products(*item) for item in items[:2]]
    sums = {}

    def add(key, value):
        sums[key] = sums[key] + value if key in sums else value

    for i, item in enumerate(items):
        member, low, key_low, r = item
        if i + 2 < len(items):
            ahead.append(products(*items[i + 2]))
        weights, grad_scores = weighted(*item, *ahead.pop(0))
        rows = head_rows(member, r)
        keys = slice(key_low, key_low + 256)
        add("value", dot(grad_ref[0, rows, low : low + BLOCK], weights, 1, 1))
        add("key", dot(query_ref[0, rows, low : low + BLOCK], grad_scores, 1, 1))
        add(r, dot(key_ref[0, member * 64 : member * 64 + 64, keys], grad_scores))
        if r == RATIO - 1:
            for name, ref in (("value", grad_value), ("key", grad_key)):
                part = sums.pop(name)
                if key_low - key_low % BLOCK == low:
                    ref[member, :, keys] = part
                else:
                    ref[member, :, keys] += part
        if key_low + 256 == low + BLOCK:
            projected_ref[0, rows, low : low + BLOCK] = turn_back(
                sums.pop(r) * HEAD_DIM ** (-0.5),
                cosine[:, low : low + BLOCK],
                sine[:, low : low + BLOCK],
            ).astype(BF16)
    for member in range(KV_HEADS):
        row = D + member * 64
        projected_ref[0, row : row + 64] = turn_back(grad_key[member], cosine, sine).astype(BF16)
        row += KV_WIDTH
        projected_ref[0, row : row + 64] = grad_value[member].astype(BF16)

    x = joined(own_ref[0], other_ref[0], info_ref[0]).astype(F32)
    normed = (x * inverse_root(x) * gain_ref[:, 0:1]).astype(BF16)
    product = dot(projected_ref[0], normed, 1, 1)

    @pl.when(step == 0)
    def _():
        weight_sums[...] = product

    @pl.when(step > 0)
    def _():
        weight_sums[...] += product

    @pl.when(step == pl.num_programs(0) - 1)
    def _():
        rows = 48
        pairs = (QKV + D) // (2 * rows)
        first = info_ref[0] == 0
        gain_sums = jnp.zeros((rows, D), F32)
        for pair in range(pairs):
            low = pair * 2 * rows
            if low < QKV:
                even, odd = weight_sums[low : low + rows], weight_sums[low + rows : low + 2 * rows]
                gain_sums = gain_sums + even * weight_ref[low : low + rows].astype(F32)
                gain_sums = gain_sums + odd * weight_ref[low + rows : low + 2 * rows].astype(F32)
            else:
                low -= QKV
                even = out_grad_ref[low : low + rows]
                odd = out_grad_ref[low + rows : low + 2 * rows]
            even, odd = even.astype(BF16), odd.astype(BF16)
            piece = info_ref[1 + 2 * pairs + pair]
            target = pl.ds(pl.multiple_of(info_ref[1 + 3 * pairs + pair], 16), rows)
            kept_ref[piece, target] = jnp.where(first, even, odd)
            sent_ref[piece, target] = jnp.where(first, odd, even)
        gain_first = jnp.sum(gain_sums, axis=0, keepdims=True) / gain_row_ref[0:1]
        tail = jnp.concatenate(
            [gain_first, gain_second_ref[...], jnp.zeros((14, D), F32)], axis=0
        ).astype(BF16)
        pieces, held, _ = kept_ref.shape
        for piece in range(pieces):
            kept_ref[piece, held - 16 :] = tail
            sent_ref[piece, held - 16 :] = tail


def attention_backward(
    info, own, other, start, gain, gain_rows, weight, out_grad, gain_second, tables, parts, pieces
):
    count = other.shape[0]
    length = 2 * other.shape[2]
    held = (pieces, (QKV + D) // (2 * pieces) + 16, D)
    projected = (count, QKV, length)
    fixed = [gain, gain_rows, weight, out_grad, gain_second, *tables]
    return pl.pallas_call(
        attention_backward_body,
        grid_spec=pltpu.PrefetchScalarGridSpec(
            num_scalar_prefetch=1,
            grid=(count,),
            in_specs=[
                pl.BlockSpec(
                    (1,) + own.shape[1:], lambda i, info: (info[0] * count + i, 0, 0)
                ),
                step_spec(other.shape),
                step_spec(start.shape),
            ]
            + [whole(part.shape) for part in fixed]
            + [step_spec(part.shape) for part in parts],
            out_specs=[step_spec(projected)] + [whole(held)] * 2,
            scratch_shapes=[
                pltpu.VMEM((KV_HEADS, length, HEAD_DIM), BF16),
                pltpu.VMEM((KV_HEADS, length, HEAD_DIM), BF16),
                pltpu.VMEM((KV_HEADS, HEAD_DIM, length), F32),
                pltpu.VMEM((KV_HEADS, HEAD_DIM, length), F32),
                pltpu.VMEM((QKV, D), F32),
            ],
        ),
        out_shape=[jax.ShapeDtypeStruct(projected, BF16)]
        + [jax.ShapeDtypeStruct(held, BF16)] * 2,
        compiler_params=params(),
        cost_estimate=pl.CostEstimate(
            flops=9_000_000_000, transcendentals=6_000_000, bytes_accessed=15_000_000
        ),
        name="attention_backward",
    )(info, own, other, start, *fixed, *parts)


def input_grads_body(
    info_ref,
    own_ref,
    other_ref,
    gain_ref,
    projected_ref,
    weight_ref,
    grad_ref,
    tokens_own_ref,
    tokens_other_ref,
):
    step = pl.program_id(0)
    x = jnp.where(step % 2 == 0, own_ref[0], other_ref[0]).astype(F32)
    gain = gain_ref[:, 0:1]
    inverse = inverse_root(x)
    normal = x * inverse
    grad_normed = dot(weight_ref[...], projected_ref[0], 0, 0)
    grad_x = grad_ref[0].astype(F32) + norm_backward(grad_normed, normal, inverse, gain)

    @pl.when(step % 2 == 0)
    def _():
        tokens_own_ref[0] = grad_x

    @pl.when(step % 2 == 1)
    def _():
        tokens_other_ref[0] = grad_x.astype(BF16)


def input_grads(info, own, other, gain, projected, weight, grad):
    count = other.shape[0]
    half = other.shape[2]
    own_spec = pl.BlockSpec((1, D, half), lambda i, info: (info[0] * count + i // 2, 0, 0))
    other_spec = pl.BlockSpec((1, D, half), lambda i, info: (i // 2, 0, 0))

    def full(height):
        return pl.BlockSpec((1, height, half), lambda i, info: (i // 2, 0, (i + info[0]) % 2))

    return pl.pallas_call(
        input_grads_body,
        grid_spec=pltpu.PrefetchScalarGridSpec(
            num_scalar_prefetch=1,
            grid=(2 * count,),
            in_specs=[
                own_spec,
                other_spec,
                whole(gain.shape),
                full(QKV),
                whole(weight.shape),
                full(D),
            ],
            out_specs=[own_spec, other_spec],
        ),
        out_shape=[
            jax.ShapeDtypeStruct(own.shape, F32),
            jax.ShapeDtypeStruct(other.shape, BF16),
        ],
        compiler_params=params(),
        cost_estimate=SHORT,
        name="input_grads",
    )(info, own, other, gain, projected, weight, grad)


def factors(count):
    inner = 1 << ((count.bit_length() - 1) // 2)
    return count // inner, inner


def partner(values, mask):
    count = lax.axis_size("wide")
    return lax.ppermute(values, "wide", [(i, i ^ mask) for i in range(count)])


def across(values):
    return lax.ppermute(values, "narrow", [(0, 1), (1, 0)])


def in_order(parts, place):
    bit = 1
    while bit < len(parts):
        swap = (place & bit) != 0
        parts = [jnp.where(swap, parts[i ^ bit], part) for i, part in enumerate(parts)]
        bit *= 2
    return parts


def add_all(parts):
    parts = [part.astype(F32) for part in parts]
    while len(parts) > 1:
        parts = [parts[i] + parts[i + 1] for i in range(0, len(parts), 2)]
    return parts[0]


def adamw_update(master, first_state, second_state, gradient, factor, step_rate, decay_rate):
    clipped = gradient * factor
    first_new = beta_first * first_state + (1.0 - beta_first) * clipped
    second_new = beta_second * second_state + (1.0 - beta_second) * clipped * clipped
    first_hat = first_new / (1.0 - beta_first**STEP)
    second_hat = second_new / (1.0 - beta_second**STEP)
    master_new = master * (1.0 - step_rate * decay_rate) - step_rate * first_hat / (
        jnp.sqrt(second_hat) + adam_epsilon
    )
    return (master_new, first_new, second_new)


def to_all(row):
    devices = lax.axis_size("wide") * lax.axis_size("narrow")
    sent = jnp.broadcast_to(row, (devices, row.shape[1]))
    return lax.all_to_all(sent, ("wide", "narrow"), 0, 0, tiled=True)


def sum_everywhere(value):
    return jnp.sum(to_all(jnp.full((1, 128), value, F32))[:, 0])


def per_device(
    tokens,
    cotangent,
    documents,
    attention_master,
    attention_first,
    attention_second,
    feedforward_master,
    feedforward_first,
    feedforward_second,
    gain_master,
    gain_first,
    gain_second,
):
    seq_count, half_len, _ = tokens.shape
    own_count = seq_count // 2
    place = lax.axis_index("narrow")
    first = place == 0
    outer, inner = factors(lax.axis_size("wide"))
    wide_place = lax.axis_index("wide")
    outer_place, inner_place = wide_place // inner, wide_place % inner
    tables = rotary_tables(2 * half_len)
    gain_columns = gain_master.T
    x_own = jnp.swapaxes(tokens, 1, 2)
    cotangent_own = jnp.swapaxes(cotangent, 1, 2)

    def swap(tensor):
        return across(jnp.where(first, tensor[own_count:], tensor[:own_count]))

    rows = attention_master.shape[0]
    aligned = rows % 16 == 0
    piece = attention_master.astype(BF16)
    parts = [piece] + [partner(piece, k * inner) for k in range(1, outer)]
    stack = jnp.stack(parts if aligned else in_order(parts, outer_place))
    parts = [stack] + [partner(stack, k) for k in range(1, inner)]
    feed_piece = feedforward_master.astype(BF16)
    feed_outer = jnp.stack(
        [feed_piece] + [partner(feed_piece, k * inner) for k in range(1, outer)]
    )
    feed_outer, parts[1:] = lax.optimization_barrier((feed_outer, parts[1:]))
    feed_parts = [feed_outer] + [partner(feed_outer, k) for k in range(1, inner)]
    if aligned:
        stack = jnp.stack(parts)
        pieces_own = stack.reshape(-1, rows, D)
        pieces_other = across(stack).reshape(-1, rows, D)
        chunk = jnp.arange(2 * inner * outer, dtype=jnp.int32)
        order = (
            ((chunk % 2) ^ place) * inner + ((chunk // 2 % inner) ^ inner_place)
        ) * outer + ((chunk // (2 * inner)) ^ outer_place)
        pair = chunk[: inner * outer]
        piece_of = (pair % inner) ^ inner_place
        row_of = ((pair // inner) ^ outer_place) * rows
        grad_pieces = inner
    else:
        stack = jnp.stack(in_order(parts, inner_place), axis=1)
        pieces = jnp.stack(in_order([stack, across(stack)], place), axis=2).reshape(-1, 48, D)
        pieces_own, pieces_other = pieces[:16], pieces[16:]
        order = jnp.arange(32, dtype=jnp.int32)
        piece_of = jnp.zeros((16,), jnp.int32)
        row_of = jnp.arange(16, dtype=jnp.int32) * 48
        grad_pieces = 1
    info = jnp.concatenate(
        [jnp.full((1,), place), order, piece_of, row_of]
    ).astype(jnp.int32)

    x_other = swap(x_own)
    own_docs = lax.dynamic_slice_in_dim(documents, place * own_count, own_count, 0)
    start = jnp.zeros_like(own_docs)
    for number in (1, 2):
        before = jnp.sum((own_docs < number).astype(jnp.int32), axis=1, keepdims=True)
        start = jnp.where(own_docs == number, before, start)
    start = start[:, None, :]

    cotangent_other = swap(cotangent_own)

    residual, query, key, value, mixed, total, weight_qkv, weight_out = attention_forward(
        info, x_own, x_other, start, pieces_own, pieces_other, gain_columns, tables
    )
    feed_parts, residual = lax.optimization_barrier((feed_parts, residual))
    if aligned:
        feed_weights = feed_parts + [across(part) for part in feed_parts]
    else:
        stack = jnp.stack(feed_parts)
        feed_weights = [
            jnp.swapaxes(part.reshape(-1, 3, rows, D), 0, 1).reshape(1, 3, -1, D)
            for part in (stack, across(stack))
        ]
    outputs, out_other, back, gain_second_part, own_grad, other_grad = feed_forward(
        info, residual, cotangent_own, cotangent_other, feed_weights, gain_columns, inner
    )

    def place_other(whole_array, received):
        return lax.dynamic_update_slice_in_dim(
            whole_array, received.astype(whole_array.dtype), (1 - place) * own_count, 0
        )

    out_received = across(out_other)

    received = across(other_grad)
    grad_mixed, inner_sums, out_grad = branch_backward(back, mixed, weight_out)
    received, own_grad, grad_mixed = lax.optimization_barrier((received, own_grad, grad_mixed))
    feed_sums = [add_all([own_grad[k], received[k]]).astype(BF16) for k in range(inner)]
    feed_sums, grad_mixed = lax.optimization_barrier((feed_sums, grad_mixed))
    feed_got = [feed_sums[0]] + [partner(feed_sums[k], k) for k in range(1, inner)]
    projected, kept, sent = attention_backward(
        info,
        x_own,
        x_other,
        start,
        gain_columns,
        gain_master,
        weight_qkv,
        out_grad,
        gain_second_part,
        tables,
        [query, key, value, total, grad_mixed, inner_sums],
        grad_pieces,
    )
    feed_got, kept, sent = lax.optimization_barrier((feed_got, kept, sent))
    summed = add_all(feed_got).astype(BF16).reshape(3, outer, -1, D)
    feed_last = [summed[:, k] for k in range(outer)]
    feed_last, sent = lax.optimization_barrier((feed_last, sent))
    feed_last = [feed_last[0]] + [partner(feed_last[k], k * inner) for k in range(1, outer)]

    received = across(sent)
    if aligned:
        parts = [add_all([kept[k], received[k]]).astype(BF16) for k in range(inner)]
    else:
        gain_grad = lax.psum(kept[0, -16:-14].astype(F32), ("wide", "narrow"))
        total = add_all([kept, received]).astype(BF16)[0, :-16].reshape(outer, inner, rows, D)
        parts = in_order([total[:, k] for k in range(inner)], inner_place)
    parts, projected = lax.optimization_barrier((parts, projected))
    got = [parts[0]] + [partner(parts[k], k) for k in range(1, inner)]
    grad_own, grad_other = input_grads(
        info, x_own, x_other, gain_columns, projected, weight_qkv, back
    )
    got, feed_last, grad_other = lax.optimization_barrier((got, feed_last, grad_other))
    total = add_all(got).astype(BF16)
    if aligned:
        tail = total[outer * rows :]
        parts = [
            jnp.concatenate([total[k * rows : (k + 1) * rows], tail], axis=0)
            for k in range(outer)
        ]
    else:
        parts = in_order([total[k] for k in range(outer)], outer_place)
    attention_grad = add_all(
        [parts[0]] + [partner(parts[k], k * inner) for k in range(1, outer)]
    )
    if aligned:
        attention_grad, gain_grad = attention_grad[:rows], attention_grad[rows : rows + 2]
    feedforward_grad = add_all(feed_last)
    grad_received = across(grad_other)
    attention_grad, gain_grad, grad_received, out_received = lax.optimization_barrier(
        (attention_grad, gain_grad, grad_received, out_received)
    )
    grad_tokens = place_other(grad_own, grad_received)
    outputs = place_other(outputs, out_received)
    local_squares = jnp.sum(attention_grad * attention_grad) + jnp.sum(
        feedforward_grad * feedforward_grad
    )
    grad_norm = jnp.sqrt(sum_everywhere(local_squares) + jnp.sum(gain_grad * gain_grad))
    factor = jnp.minimum(1.0, clip_limit / (grad_norm + 1e-06))
    update = functools.partial(adamw_update, factor=factor)
    attention_new = update(
        attention_master,
        attention_first,
        attention_second,
        attention_grad,
        step_rate=rate_matrix,
        decay_rate=weight_decay,
    )
    feedforward_new = update(
        feedforward_master,
        feedforward_first,
        feedforward_second,
        feedforward_grad,
        step_rate=rate_matrix,
        decay_rate=weight_decay,
    )
    gain_new = update(
        gain_master, gain_first, gain_second, gain_grad, step_rate=rate_gain, decay_rate=0.0
    )
    outputs = jnp.swapaxes(outputs, 1, 2)
    grad_tokens = jnp.swapaxes(grad_tokens, 1, 2)
    return (outputs, grad_tokens, grad_norm, *attention_new, *feedforward_new, *gain_new)


def solution(mesh):
    sequences = P("wide", "narrow", None)
    attention = P(("wide", "narrow"), None)
    feedforward = P(None, ("narrow", "wide"), None)
    state = (attention,) * 3 + (feedforward,) * 3 + (P(),) * 3
    return jax.shard_map(
        per_device,
        mesh=mesh,
        in_specs=(sequences, sequences, P("wide", None)) + state,
        out_specs=(sequences, sequences, P()) + state,
        check_vma=False,
    )
```

profile of v0, /device:TPU:0, one launch (start us, length us, event | category | flops | bytes accessed | tf_op | source)
XLA Modules:
  0.0 240.5 jit_solution(16653151287299238956)
XLA Ops:
  0.6 0.9 convert_element_type.182
  1.6 4.1 %collective-permute-start.4 = (bf16[48,576]{1,0:T(8,128)(2,1)S(1)}, bf16[48,576]{1,0:T(8,128)(2,1)S(1)}, u32[]{:S(2)}, u32[]{:S(2)}) collective-permute-start(bf16[48,576]{1,0:T(8,128)(2,1)S(1)} %convert_element_type.182), channel_id=1, source_target_pairs={{0,16},{2,18},{4,20},{6,22},{8,24},{10,26},{12,28},{14,30},{16,0},... | collective-permute-start | bytes 165896 | tf_op jit(solution)/shard_map/ppermute | solution.py:673
  5.7 1.6 collective-permute-start.3
  7.2 1.0 convert_element_type.181
  8.2 2.0 collective-permute-start.1
  10.2 2.5 %collective-permute-start = (bf16[3,48,576]{2,1,0:T(8,128)(2,1)S(1)}, bf16[3,48,576]{2,1,0:T(8,128)(2,1)S(1)}, u32[]{:S(2)}, u32[]{:S(2)}) collective-permute-start(bf16[3,48,576]{2,1,0:T(8,128)(2,1)S(1)} %convert_element_type.181), channel_id=1, source_target_pairs={{0,8},{2,10},{4,12},{6,14},{8,0},{10,2},{12,4},{14,6},{16,24},{18,... | collective-permute-start | bytes 497672 | tf_op jit(solution)/shard_map/ppermute | solution.py:673
  12.7 2.8 %slice_select_fusion.1 = bf16[2,576,512]{2,1,0:T(8,128)(2,1)} fusion(bf16[4,576,512]{2,1,0:T(8,128)(2,1)} %bitcast.57, pred[]{:T(512)S(6)} %eq.16), kind=kLoop, calls=%fused_computation.7 | loop fusion | flops 589824 | bytes 3538945 | tf_op jit(solution)/shard_map/jit(_where)/select_n | solution.py:745
  15.5 1.4 collective-permute-start.2
  17.0 2.5 %collective-permute-start.8 = (bf16[4,48,576]{2,1,0:T(8,128)(2,1)S(1)}, bf16[4,48,576]{2,1,0:T(8,128)(2,1)S(1)}, u32[]{:S(2)}, u32[]{:S(2)}) collective-permute-start(bf16[4,48,576]{2,1,0:T(8,128)(2,1)S(1)} %get-tuple-element.175), channel_id=1, source_target_pairs={{0,6},{2,4},{4,2},{6,0},{8,14},{10,12},{12,10},{14,8},{16,22},{18,... | collective-permute-start | bytes 663560 | tf_op jit(solution)/shard_map/ppermute | solution.py:673
  19.5 0.5 collective-permute-start.7
  20.0 4.9 %collective-permute-done.1 = bf16[3,48,576]{2,1,0:T(8,128)(2,1)S(1)} collective-permute-done((bf16[3,48,576]{2,1,0:T(8,128)(2,1)S(1)}, bf16[3,48,576]{2,1,0:T(8,128)(2,1)S(1)}, u32[]{:S(2)}, u32[]{:S(2)}) %collective-permute-start.1) | collective-permute-done | bytes 165920 | tf_op jit(solution)/shard_map/ppermute | solution.py:673
  24.9 1.5 collective-permute-start.6
  26.7 1.5 collective-permute-done.7
  28.2 2.9 %collective-permute-done.6 = bf16[4,48,576]{2,1,0:T(8,128)(2,1)S(1)} collective-permute-done((bf16[4,48,576]{2,1,0:T(8,128)(2,1)S(1)}, bf16[4,48,576]{2,1,0:T(8,128)(2,1)S(1)}, u32[]{:S(2)}, u32[]{:S(2)}) %collective-permute-start.6) | collective-permute-done | bytes 221216 | tf_op jit(solution)/shard_map/ppermute | solution.py:673
  31.1 1.2 pad_maximum_fusion
  32.3 1.2 slice_select_fusion
  34.2 0.6 broadcast_in_dim.28.start_ref
  34.8 0.9 copy.36
  35.7 0.6 pad_add_fusion.info_ref
  36.3 2.4 %collective-permute-start.11 = (bf16[4,3,48,576]{3,2,1,0:T(8,128)(2,1)S(1)}, bf16[4,3,48,576]{3,2,1,0:T(8,128)(2,1)}, u32[]{:S(2)}, u32[]{:S(2)}) collective-permute-start(bf16[4,3,48,576]{3,2,1,0:T(8,128)(2,1)S(1)} %pad_maximum_fusion.1.refs_0_), channel_id=1, source_target_pairs={{0,6},{2,4},{4,2},{6,0},{8,14},{10,12},{12,10},{14,8},{16,22},{18,... | collective-permute-start | bytes 1990664 | tf_op jit(solution)/shard_map/ppermute | solution.py:673
  38.8 0.5 collective-permute-start.10
  39.3 0.5 collective-permute-start.9
  40.2 27.3 %attention_forward.1 = (f32[2,576,1024]{2,1,0:T(8,128)}, bf16[2,576,1024]{2,1,0:T(8,128)(2,1)}, bf16[2,192,1024]{2,1,0:T(8,128)(2,1)}, bf16[2,192,1024]{2,1,0:T(...) custom-call(s32[65]{0:T(128)} %pad_add_fusion.info_ref, ...), custom_call_target="tpu_custom_call" | custom-call | flops 8000000000 | bytes 20000000 | tf_op jit(solution)/shard_map/attention_forward/pallas_call | solution.py:226
  67.6 3.9 %collective-permute-done.10.refs_2_ = bf16[4,3,48,576]{3,2,1,0:T(8,128)(2,1)} collective-permute-done((bf16[4,3,48,576]{3,2,1,0:T(8,128)(2,1)S(1)}, bf16[4,3,48,576]{3,2,1,0:T(8,128)(2,1)}, u32[]{:S(2)}, u32[]{:S(2)}) %collective-permute-start.10) | collective-permute-done | bytes 663584 | tf_op jit(solution)/shard_map/ppermute | solution.py:673
  71.6 0.5 collective-permute-start.16
  72.1 0.5 collective-permute-start.18
  72.7 2.2 collective-permute-done.15.refs_4_
  75.2 1.1 collective-permute-done.17.refs_6_
  76.3 1.1 collective-permute-done.18.refs_7_
  77.4 54.7 %feed_forward.1 = (bf16[4,576,512]{2,1,0:T(8,128)(2,1)}, bf16[2,576,512]{2,1,0:T(8,128)(2,1)}, bf16[2,576,1024]{2,1,0:T(8,128)(2,1)}, f32[1,576]{1,0:T(1,128)}, ...) custom-call(s32[65]{0:T(128)} %pad_add_fusion.info_ref, ...), custom_call_target="tpu_custom_call" | custom-call | flops 32000000000 | bytes 30000000 | tf_op jit(solution)/shard_map/feed_forward/pallas_call | solution.py:349
  132.3 7.7 %branch_backward.1 = (bf16[2,576,1024]{2,1,0:T(8,128)(2,1)}, f32[2,3,8,1024]{3,2,1,0:T(8,128)}, f32[576,576]{1,0:T(8,128)}) custom-call(bf16[2,576,1024]{2,1,0:T(8,128)(2,1)} %get-tuple-element.93.grad_ref, bf16[2,576,1024]{2,1,0:T(8,128)(2,1)} %get-tuple-element.94.mixed_ref, bf16[576,576]{1,0:T(8,128)(2,1)} %get-tuple-element.95.weight_ref), custom_call_target="tpu_custom_call" | custom-call | flops 1000000 | bytes 100000 | tf_op jit(solution)/shard_map/branch_backward/pallas_call | solution.py:402
  139.9 3.9 %fusion.3 = (bf16[3,192,576]{2,1,0:T(8,128)(2,1)}, bf16[3,192,576]{2,1,0:T(8,128)(2,1)}, bf16[3,192,576]{2,1,0:T(8,128)(2,1)}, bf16[3,192,576]{2,1,0:T(8,128)(2,1)S(1)}) fusion(bf16[4,3,192,576]{3,2,1,0:T(8,128)(2,1)} %collective-permute-done.19, bf16[4,3,192,576]{3,2,1,0:T(8,128)(2,1)S(1)} %copy-done.1), kind=kLoop, calls=%fused_computation.12 | loop fusion | flops 5308416 | bytes 7962624 | tf_op jit(solution)/shard_map/convert_element_type | solution.py:819
  143.9 1.5 collective-permute-start.20
  145.4 0.7 collective-permute-start.21
  146.1 1.3 collective-permute-start.22
  147.4 36.0 %attention_backward.1 = (bf16[2,960,1024]{2,1,0:T(8,128)(2,1)}, bf16[4,208,576]{2,1,0:T(8,128)(2,1)}, bf16[4,208,576]{2,1,0:T(8,128)(2,1)}) custom-call(s32[65]{0:T(128)} %pad_add_fusion.info_ref, bf16[4,576,512]{2,1,0:T(8,128)(2,1)} %bitcast.59, bf16[2,576,512]{2,1,0:T(8,128)(2,1)} %collective-permute-done.12.other_ref, ...), custom_call_target="tpu_custom_call" | custom-call | flops 8999999488 | bytes 15000000 | tf_op jit(solution)/shard_map/attention_backward/pallas_call | solution.py:571
  183.9 0.8 copy-done.20
  184.6 2.7 %collective-permute-done.23 = bf16[4,208,576]{2,1,0:T(8,128)(2,1)S(1)} collective-permute-done((bf16[4,208,576]{2,1,0:T(8,128)(2,1)S(1)}, bf16[4,208,576]{2,1,0:T(8,128)(2,1)S(1)}, u32[]{:S(2)}, u32[]{:S(2)}) %collective-permute-start.23) | collective-permute-done | bytes 958496 | tf_op jit(solution)/shard_map/ppermute | solution.py:677
  187.6 1.6 collective-permute-start.24
  189.2 0.7 collective-permute-start.25
  189.9 1.3 collective-permute-start.26
  191.1 1.3 collective-permute-start.28
  192.4 2.6 %collective-permute-start.29 = (bf16[3,48,576]{2,1,0:T(8,128)(2,1)S(1)}, bf16[3,48,576]{2,1,0:T(8,128)(2,1)S(1)}, u32[]{:S(2)}, u32[]{:S(2)}) collective-permute-start(bf16[3,48,576]{2,1,0:T(8,128)(2,1)S(1)} %get-tuple-element.130), channel_id=1, source_target_pairs={{0,24},{2,26},{4,28},{6,30},{8,16},{10,18},{12,20},{14,22},{16,8},... | collective-permute-start | bytes 497672 | tf_op jit(solution)/shard_map/ppermute | solution.py:673
  195.1 10.3 %input_grads.1 = (f32[4,576,512]{2,1,0:T(8,128)}, bf16[2,576,512]{2,1,0:T(8,128)(2,1)}) custom-call(s32[65]{0:T(128)} %pad_add_fusion.info_ref, bf16[4,576,512]{2,1,0:T(8,128)(2,1)} %bitcast.60, bf16[2,576,512]{2,1,0:T(8,128)(2,1)} %collective-permute-done.12.other_ref, f32[576,2]{1,0:T(8,128)} %bitcast.67, ...), custom_call_target="tpu_custom_call" | custom-call | flops 1000000 | bytes 100000 | tf_op jit(solution)/shard_map/input_grads/pallas_call | solution.py:641
  205.4 1.3 collective-permute-done.28
  206.8 0.6 copy-done.7
  208.1 1.3 add_convert_fusion.5
  209.4 1.5 collective-permute-start.32
  210.9 3.1 %collective-permute-start.30 = (bf16[64,576]{1,0:T(8,128)(2,1)S(1)}, bf16[64,576]{1,0:T(8,128)(2,1)S(1)}, u32[]{:S(2)}, u32[]{:S(2)}) collective-permute-start(bf16[64,576]{1,0:T(8,128)(2,1)S(1)} %get-tuple-element.176), channel_id=1, source_target_pairs={{0,8},{2,10},{4,12},{6,14},{8,0},{10,2},{12,4},{14,6},{16,24},{18,... | collective-permute-start | bytes 221192 | tf_op jit(solution)/shard_map/ppermute | solution.py:673
  214.2 0.7 multiply_reduce_fusion
  214.9 0.8 collective-permute-done.32
  215.8 1.7 collective-permute-done.30
  217.5 3.5 %collective-permute-done.31 = bf16[64,576]{1,0:T(8,128)(2,1)S(1)} collective-permute-done((bf16[64,576]{1,0:T(8,128)(2,1)S(1)}, bf16[64,576]{1,0:T(8,128)(2,1)S(1)}, u32[]{:S(2)}, u32[]{:S(2)}) %collective-permute-start.31) | collective-permute-done | bytes 73760 | tf_op jit(solution)/shard_map/ppermute | solution.py:673
  221.1 0.6 multiply_reduce_fusion.1
  223.0 0.6 broadcast_in_dim_broadcast_in_dim.3
  223.6 3.1 %all-to-all-start = ((f32[32,1,128]{2,1,0:T(1,128)}), f32[32,1,128]{2,1,0:T(1,128)S(1)}, u32[]{:S(2)}, u32[]{:S(2)}) async-start(f32[32,1,128]{2,1,0:T(1,128)} %broadcast_in_dim_broadcast_in_dim.3), calls=%async_computation | async-start | bytes 32768 | tf_op jit(solution)/shard_map/all_to_all | solution.py:711
  226.7 1.1 constant_dynamic-update-slice_fusion
  227.9 1.7 convert_dynamic-update-slice_fusion
  229.6 0.6 multiply_reduce_fusion.2
  230.2 3.6 %all-to-all-done = f32[32,1,128]{2,1,0:T(1,128)S(1)} async-done(((f32[32,1,128]{2,1,0:T(1,128)}), f32[32,1,128]{2,1,0:T(1,128)S(1)}, u32[]{:S(2)}, u32[]{:S(2)}) %all-to-all-start) | async-done | bytes 16416 | tf_op jit(solution)/shard_map/all_to_all | solution.py:711
  233.8 0.6 slice_reduce_fusion
  235.8 1.3 divide_subtract_fusion.2
  237.1 0.8 divide_subtract_fusion.1
  237.9 1.2 divide_subtract_fusion
  (98 shorter events, 4.0 us)
Async XLA Ops:
  1.6 14.0 %collective-permute-start.4 = (bf16[48,576]{1,0:T(8,128)(2,1)S(1)}, bf16[48,576]{1,0:T(8,128)(2,1)S(1)}, u32[]{:S(2)}, u32[]{:S(2)}) collective-permute-start(bf16[48,576]{1,0:T(8,128)(2,1)S(1)} %convert_element_type.182), channel_id=1, source_target_pairs={{0,16},{2,18},{4,20},{6,22},{8,24},{10,26},{12,28},{14,30},{16,0},... | collective-permute-start | bytes 165896 | tf_op jit(solution)/shard_map/ppermute | solution.py:673
  5.7 11.3 %collective-permute-start.3 = (bf16[48,576]{1,0:T(8,128)(2,1)S(1)}, bf16[48,576]{1,0:T(8,128)(2,1)S(1)}, u32[]{:S(2)}, u32[]{:S(2)}) collective-permute-start(bf16[48,576]{1,0:T(8,128)(2,1)S(1)} %convert_element_type.182), channel_id=1, source_target_pairs={{0,8},{2,10},{4,12},{6,14},{8,0},{10,2},{12,4},{14,6},{16,24},{18,... | collective-permute-start | bytes 165896 | tf_op jit(solution)/shard_map/ppermute | solution.py:673
  7.2 9.7 %collective-permute-start.5 = (bf16[48,576]{1,0:T(8,128)(2,1)S(1)}, bf16[48,576]{1,0:T(8,128)(2,1)S(1)}, u32[]{:S(2)}, u32[]{:S(2)}) collective-permute-start(bf16[48,576]{1,0:T(8,128)(2,1)S(1)} %convert_element_type.182), channel_id=1, source_target_pairs={{0,24},{2,26},{4,28},{6,30},{8,16},{10,18},{12,20},{14,22},{16,8},... | collective-permute-start | bytes 165896 | tf_op jit(solution)/shard_map/ppermute | solution.py:673
  8.2 16.6 %collective-permute-start.1 = (bf16[3,48,576]{2,1,0:T(8,128)(2,1)S(1)}, bf16[3,48,576]{2,1,0:T(8,128)(2,1)S(1)}, u32[]{:S(2)}, u32[]{:S(2)}) collective-permute-start(bf16[3,48,576]{2,1,0:T(8,128)(2,1)S(1)} %convert_element_type.181), channel_id=1, source_target_pairs={{0,16},{2,18},{4,20},{6,22},{8,24},{10,26},{12,28},{14,30},{16,0},... | collective-permute-start | bytes 497672 | tf_op jit(solution)/shard_map/ppermute | solution.py:673
  10.2 16.2 %collective-permute-start = (bf16[3,48,576]{2,1,0:T(8,128)(2,1)S(1)}, bf16[3,48,576]{2,1,0:T(8,128)(2,1)S(1)}, u32[]{:S(2)}, u32[]{:S(2)}) collective-permute-start(bf16[3,48,576]{2,1,0:T(8,128)(2,1)S(1)} %convert_element_type.181), channel_id=1, source_target_pairs={{0,8},{2,10},{4,12},{6,14},{8,0},{10,2},{12,4},{14,6},{16,24},{18,... | collective-permute-start | bytes 497672 | tf_op jit(solution)/shard_map/ppermute | solution.py:673
  12.7 2.8 %copy-start.3 = (f32[48,576]{1,0:T(8,128)S(1)}, f32[48,576]{1,0:T(8,128)}, u32[]{:S(2)}) copy-start(f32[48,576]{1,0:T(8,128)} %param.17) | copy-start | bytes 331780
  12.7 13.7 %copy-start = (f32[3,48,576]{2,1,0:T(8,128)S(1)}, f32[3,48,576]{2,1,0:T(8,128)}, u32[]{:S(2)}) copy-start(f32[3,48,576]{2,1,0:T(8,128)} %param.20) | copy-start | bytes 995332
  15.5 11.0 %collective-permute-start.2 = (bf16[3,48,576]{2,1,0:T(8,128)(2,1)S(1)}, bf16[3,48,576]{2,1,0:T(8,128)(2,1)S(1)}, u32[]{:S(2)}, u32[]{:S(2)}) collective-permute-start(bf16[3,48,576]{2,1,0:T(8,128)(2,1)S(1)} %convert_element_type.181), channel_id=1, source_target_pairs={{0,24},{2,26},{4,28},{6,30},{8,16},{10,18},{12,20},{14,22},{16,8},... | collective-permute-start | bytes 497672 | tf_op jit(solution)/shard_map/ppermute | solution.py:673
  17.0 9.7 %collective-permute-start.8 = (bf16[4,48,576]{2,1,0:T(8,128)(2,1)S(1)}, bf16[4,48,576]{2,1,0:T(8,128)(2,1)S(1)}, u32[]{:S(2)}, u32[]{:S(2)}) collective-permute-start(bf16[4,48,576]{2,1,0:T(8,128)(2,1)S(1)} %get-tuple-element.175), channel_id=1, source_target_pairs={{0,6},{2,4},{4,2},{6,0},{8,14},{10,12},{12,10},{14,8},{16,22},{18,... | collective-permute-start | bytes 663560 | tf_op jit(solution)/shard_map/ppermute | solution.py:673
  19.5 8.7 %collective-permute-start.7 = (bf16[4,48,576]{2,1,0:T(8,128)(2,1)S(1)}, bf16[4,48,576]{2,1,0:T(8,128)(2,1)S(1)}, u32[]{:S(2)}, u32[]{:S(2)}) collective-permute-start(bf16[4,48,576]{2,1,0:T(8,128)(2,1)S(1)} %get-tuple-element.175), channel_id=1, source_target_pairs={{0,4},{2,6},{4,0},{6,2},{8,12},{10,14},{12,8},{14,10},{16,20},{18,... | collective-permute-start | bytes 663560 | tf_op jit(solution)/shard_map/ppermute | solution.py:673
  24.9 6.2 %collective-permute-start.6 = (bf16[4,48,576]{2,1,0:T(8,128)(2,1)S(1)}, bf16[4,48,576]{2,1,0:T(8,128)(2,1)S(1)}, u32[]{:S(2)}, u32[]{:S(2)}) collective-permute-start(bf16[4,48,576]{2,1,0:T(8,128)(2,1)S(1)} %get-tuple-element.175), channel_id=1, source_target_pairs={{0,2},{2,0},{4,6},{6,4},{8,10},{10,8},{12,14},{14,12},{16,18},{18,... | collective-permute-start | bytes 663560 | tf_op jit(solution)/shard_map/ppermute | solution.py:673
  26.4 13.4 %collective-permute-start.12 = (bf16[2,576,512]{2,1,0:T(8,128)(2,1)}, bf16[2,576,512]{2,1,0:T(8,128)(2,1)}, u32[]{:S(2)}, u32[]{:S(2)}) collective-permute-start(bf16[2,576,512]{2,1,0:T(8,128)(2,1)} %slice_select_fusion.1), channel_id=1, source_target_pairs={{0,1},{1,0},{2,3},{3,2},{4,5},{5,4},{6,7},{7,6},{8,9},{9,8},{10,11... | collective-permute-start | bytes 3538952 | tf_op jit(solution)/shard_map/ppermute | solution.py:677
  26.5 5.8 %copy-start.2 = (bf16[4,512,576]{1,2,0:T(8,128)(2,1)S(1)}, bf16[4,512,576]{1,2,0:T(8,128)(2,1)}, u32[]{:S(2)}) copy-start(bf16[4,512,576]{1,2,0:T(8,128)(2,1)} %param.15) | copy-start | bytes 7077892
  26.7 45.0 %copy-start.6 = (bf16[4,3,48,576]{3,2,1,0:T(8,128)(2,1)}, bf16[4,3,48,576]{3,2,1,0:T(8,128)(2,1)S(1)}, u32[]{:S(2)}) copy-start(bf16[4,3,48,576]{3,2,1,0:T(8,128)(2,1)S(1)} %pad_maximum_fusion.1.refs_0_) | copy-start | bytes 1990660
  32.3 7.0 %collective-permute-start.13 = (bf16[4,4,48,576]{3,2,1,0:T(8,128)(2,1)}, bf16[4,4,48,576]{3,2,1,0:T(8,128)(2,1)S(1)}, u32[]{:S(2)}, u32[]{:S(2)}) collective-permute-start(bf16[4,4,48,576]{3,2,1,0:T(8,128)(2,1)} %pad_maximum_fusion), channel_id=1, source_target_pairs={{0,1},{1,0},{2,3},{3,2},{4,5},{5,4},{6,7},{7,6},{8,9},{9,8},{10,11... | collective-permute-start | bytes 2654216 | tf_op jit(solution)/shard_map/ppermute | solution.py:677
  32.3 1.7 copy-start.18
  32.3 2.5 %copy-start.16 = (f32[2,576]{1,0:T(2,128)S(1)}, f32[2,576]{1,0:T(2,128)}, u32[]{:S(2)}) copy-start(f32[2,576]{1,0:T(2,128)} %gain_row_ref.1) | copy-start | bytes 13828
  33.5 39.2 %collective-permute-start.14 = (bf16[2,576,512]{2,1,0:T(8,128)(2,1)}, bf16[2,576,512]{2,1,0:T(8,128)(2,1)S(1)}, u32[]{:S(2)}, u32[]{:S(2)}) collective-permute-start(bf16[2,576,512]{2,1,0:T(8,128)(2,1)} %slice_select_fusion), channel_id=1, source_target_pairs={{0,1},{1,0},{2,3},{3,2},{4,5},{5,4},{6,7},{7,6},{8,9},{9,8},{10,11... | collective-permute-start | bytes 3538952 | tf_op jit(solution)/shard_map/ppermute | solution.py:677
  36.3 31.3 %collective-permute-start.11 = (bf16[4,3,48,576]{3,2,1,0:T(8,128)(2,1)S(1)}, bf16[4,3,48,576]{3,2,1,0:T(8,128)(2,1)}, u32[]{:S(2)}, u32[]{:S(2)}) collective-permute-start(bf16[4,3,48,576]{3,2,1,0:T(8,128)(2,1)S(1)} %pad_maximum_fusion.1.refs_0_), channel_id=1, source_target_pairs={{0,6},{2,4},{4,2},{6,0},{8,14},{10,12},{12,10},{14,8},{16,22},{18,... | collective-permute-start | bytes 1990664 | tf_op jit(solution)/shard_map/ppermute | solution.py:673
  38.8 32.8 %collective-permute-start.10 = (bf16[4,3,48,576]{3,2,1,0:T(8,128)(2,1)S(1)}, bf16[4,3,48,576]{3,2,1,0:T(8,128)(2,1)}, u32[]{:S(2)}, u32[]{:S(2)}) collective-permute-start(bf16[4,3,48,576]{3,2,1,0:T(8,128)(2,1)S(1)} %pad_maximum_fusion.1.refs_0_), channel_id=1, source_target_pairs={{0,4},{2,6},{4,0},{6,2},{8,12},{10,14},{12,8},{14,10},{16,20},{18,... | collective-permute-start | bytes 1990664 | tf_op jit(solution)/shard_map/ppermute | solution.py:673
  39.3 0.9 copy-start.21
  39.3 32.3 %collective-permute-start.9 = (bf16[4,3,48,576]{3,2,1,0:T(8,128)(2,1)S(1)}, bf16[4,3,48,576]{3,2,1,0:T(8,128)(2,1)}, u32[]{:S(2)}, u32[]{:S(2)}) collective-permute-start(bf16[4,3,48,576]{3,2,1,0:T(8,128)(2,1)S(1)} %pad_maximum_fusion.1.refs_0_), channel_id=1, source_target_pairs={{0,2},{2,0},{4,6},{6,4},{8,10},{10,8},{12,14},{14,12},{16,18},{18,... | collective-permute-start | bytes 1990664 | tf_op jit(solution)/shard_map/ppermute | solution.py:673
  71.6 3.2 %collective-permute-start.15 = (bf16[4,3,48,576]{3,2,1,0:T(8,128)(2,1)S(1)}, bf16[4,3,48,576]{3,2,1,0:T(8,128)(2,1)S(1)}, u32[]{:S(2)}, u32[]{:S(2)}) collective-permute-start(bf16[4,3,48,576]{3,2,1,0:T(8,128)(2,1)S(1)} %pad_maximum_fusion.1.refs_0_), channel_id=1, source_target_pairs={{0,1},{1,0},{2,3},{3,2},{4,5},{5,4},{6,7},{7,6},{8,9},{9,8},{10,11... | collective-permute-start | bytes 1990664 | tf_op jit(solution)/shard_map/ppermute | solution.py:677
  71.6 3.6 %collective-permute-start.16 = (bf16[4,3,48,576]{3,2,1,0:T(8,128)(2,1)}, bf16[4,3,48,576]{3,2,1,0:T(8,128)(2,1)}, u32[]{:S(2)}, u32[]{:S(2)}) collective-permute-start(bf16[4,3,48,576]{3,2,1,0:T(8,128)(2,1)} %collective-permute-done.9.refs_1_), channel_id=1, source_target_pairs={{0,1},{1,0},{2,3},{3,2},{4,5},{5,4},{6,7},{7,6},{8,9},{9,8},{10,11... | collective-permute-start | bytes 1990664 | tf_op jit(solution)/shard_map/ppermute | solution.py:677
  72.1 4.2 %collective-permute-start.17 = (bf16[4,3,48,576]{3,2,1,0:T(8,128)(2,1)}, bf16[4,3,48,576]{3,2,1,0:T(8,128)(2,1)}, u32[]{:S(2)}, u32[]{:S(2)}) collective-permute-start(bf16[4,3,48,576]{3,2,1,0:T(8,128)(2,1)} %collective-permute-done.10.refs_2_), channel_id=1, source_target_pairs={{0,1},{1,0},{2,3},{3,2},{4,5},{5,4},{6,7},{7,6},{8,9},{9,8},{10,11... | collective-permute-start | bytes 1990664 | tf_op jit(solution)/shard_map/ppermute | solution.py:677
  72.1 5.2 %collective-permute-start.18 = (bf16[4,3,48,576]{3,2,1,0:T(8,128)(2,1)}, bf16[4,3,48,576]{3,2,1,0:T(8,128)(2,1)}, u32[]{:S(2)}, u32[]{:S(2)}) collective-permute-start(bf16[4,3,48,576]{3,2,1,0:T(8,128)(2,1)} %collective-permute-done.11.refs_3_), channel_id=1, source_target_pairs={{0,1},{1,0},{2,3},{3,2},{4,5},{5,4},{6,7},{7,6},{8,9},{9,8},{10,11... | collective-permute-start | bytes 1990664 | tf_op jit(solution)/shard_map/ppermute | solution.py:677
  72.7 4.7 %copy-start.19 = (bf16[2,576,512]{2,1,0:T(8,128)(2,1)}, bf16[2,576,512]{2,1,0:T(8,128)(2,1)S(1)}, u32[]{:S(2)}) copy-start(bf16[2,576,512]{2,1,0:T(8,128)(2,1)S(1)} %collective-permute-done.14.cotangent_other_ref) | copy-start | bytes 3538948
  74.9 2.5 %copy-start.22 = (bf16[4,3,48,576]{3,2,1,0:T(8,128)(2,1)}, bf16[4,3,48,576]{3,2,1,0:T(8,128)(2,1)S(1)}, u32[]{:S(2)}) copy-start(bf16[4,3,48,576]{3,2,1,0:T(8,128)(2,1)S(1)} %collective-permute-done.15.refs_4_) | copy-start | bytes 1990660
  132.1 7.9 %collective-permute-start.19 = (bf16[4,3,192,576]{3,2,1,0:T(8,128)(2,1)}, bf16[4,3,192,576]{3,2,1,0:T(8,128)(2,1)}, u32[]{:S(2)}, u32[]{:S(2)}) collective-permute-start(bf16[4,3,192,576]{3,2,1,0:T(8,128)(2,1)} %get-tuple-element.91), channel_id=1, source_target_pairs={{0,1},{1,0},{2,3},{3,2},{4,5},{5,4},{6,7},{7,6},{8,9},{9,8},{10,11... | collective-permute-start | bytes 7962632 | tf_op jit(solution)/shard_map/ppermute | solution.py:677
  132.3 7.7 %copy-start.1 = (bf16[4,3,192,576]{3,2,1,0:T(8,128)(2,1)S(1)}, bf16[4,3,192,576]{3,2,1,0:T(8,128)(2,1)}, u32[]{:S(2)}) copy-start(bf16[4,3,192,576]{3,2,1,0:T(8,128)(2,1)} %get-tuple-element.97) | copy-start | bytes 7962628
  143.9 39.5 %collective-permute-start.20 = (bf16[3,192,576]{2,1,0:T(8,128)(2,1)}, bf16[3,192,576]{2,1,0:T(8,128)(2,1)S(1)}, u32[]{:S(2)}, u32[]{:S(2)}) collective-permute-start(bf16[3,192,576]{2,1,0:T(8,128)(2,1)} %get-tuple-element.101), channel_id=1, source_target_pairs={{0,2},{2,0},{4,6},{6,4},{8,10},{10,8},{12,14},{14,12},{16,18},{18,... | collective-permute-start | bytes 1990664 | tf_op jit(solution)/shard_map/ppermute | solution.py:673
  145.4 38.0 %collective-permute-start.21 = (bf16[3,192,576]{2,1,0:T(8,128)(2,1)}, bf16[3,192,576]{2,1,0:T(8,128)(2,1)S(1)}, u32[]{:S(2)}, u32[]{:S(2)}) collective-permute-start(bf16[3,192,576]{2,1,0:T(8,128)(2,1)} %get-tuple-element.102), channel_id=1, source_target_pairs={{0,4},{2,6},{4,0},{6,2},{8,12},{10,14},{12,8},{14,10},{16,20},{18,... | collective-permute-start | bytes 1990664 | tf_op jit(solution)/shard_map/ppermute | solution.py:673
  146.1 37.3 %collective-permute-start.22 = (bf16[3,192,576]{2,1,0:T(8,128)(2,1)}, bf16[3,192,576]{2,1,0:T(8,128)(2,1)S(1)}, u32[]{:S(2)}, u32[]{:S(2)}) collective-permute-start(bf16[3,192,576]{2,1,0:T(8,128)(2,1)} %get-tuple-element.103), channel_id=1, source_target_pairs={{0,6},{2,4},{4,2},{6,0},{8,14},{10,12},{12,10},{14,8},{16,22},{18,... | collective-permute-start | bytes 1990664 | tf_op jit(solution)/shard_map/ppermute | solution.py:673
  183.4 1.2 copy-start.20
  183.8 3.5 %copy-start.5 = (bf16[4,208,576]{2,1,0:T(8,128)(2,1)S(1)}, bf16[4,208,576]{2,1,0:T(8,128)(2,1)}, u32[]{:S(2)}) copy-start(bf16[4,208,576]{2,1,0:T(8,128)(2,1)} %get-tuple-element.115) | copy-start | bytes 2875396
  184.6 2.7 %collective-permute-start.23 = (bf16[4,208,576]{2,1,0:T(8,128)(2,1)S(1)}, bf16[4,208,576]{2,1,0:T(8,128)(2,1)S(1)}, u32[]{:S(2)}, u32[]{:S(2)}) collective-permute-start(bf16[4,208,576]{2,1,0:T(8,128)(2,1)S(1)} %copy-done.20), channel_id=1, source_target_pairs={{0,1},{1,0},{2,3},{3,2},{4,5},{5,4},{6,7},{7,6},{8,9},{9,8},{10,11... | collective-permute-start | bytes 2875400 | tf_op jit(solution)/shard_map/ppermute | solution.py:677
  184.6 7.8 %collective-permute-start.27 = (bf16[3,48,576]{2,1,0:T(8,128)(2,1)S(1)}, bf16[3,48,576]{2,1,0:T(8,128)(2,1)S(1)}, u32[]{:S(2)}, u32[]{:S(2)}) collective-permute-start(bf16[3,48,576]{2,1,0:T(8,128)(2,1)S(1)} %get-tuple-element.128), channel_id=1, source_target_pairs={{0,8},{2,10},{4,12},{6,14},{8,0},{10,2},{12,4},{14,6},{16,24},{18,... | collective-permute-start | bytes 497672 | tf_op jit(solution)/shard_map/ppermute | solution.py:673
  187.6 19.1 %collective-permute-start.24 = (bf16[208,576]{1,0:T(8,128)(2,1)S(1)}, bf16[208,576]{1,0:T(8,128)(2,1)S(1)}, u32[]{:S(2)}, u32[]{:S(2)}) collective-permute-start(bf16[208,576]{1,0:T(8,128)(2,1)S(1)} %get-tuple-element.124), channel_id=1, source_target_pairs={{0,2},{2,0},{4,6},{6,4},{8,10},{10,8},{12,14},{14,12},{16,18},{18,... | collective-permute-start | bytes 718856 | tf_op jit(solution)/shard_map/ppermute | solution.py:673
  189.2 17.6 %collective-permute-start.25 = (bf16[208,576]{1,0:T(8,128)(2,1)S(1)}, bf16[208,576]{1,0:T(8,128)(2,1)S(1)}, u32[]{:S(2)}, u32[]{:S(2)}) collective-permute-start(bf16[208,576]{1,0:T(8,128)(2,1)S(1)} %get-tuple-element.125), channel_id=1, source_target_pairs={{0,4},{2,6},{4,0},{6,2},{8,12},{10,14},{12,8},{14,10},{16,20},{18,... | collective-permute-start | bytes 718856 | tf_op jit(solution)/shard_map/ppermute | solution.py:673
  189.9 16.9 %collective-permute-start.26 = (bf16[208,576]{1,0:T(8,128)(2,1)S(1)}, bf16[208,576]{1,0:T(8,128)(2,1)}, u32[]{:S(2)}, u32[]{:S(2)}) collective-permute-start(bf16[208,576]{1,0:T(8,128)(2,1)S(1)} %get-tuple-element.126), channel_id=1, source_target_pairs={{0,6},{2,4},{4,2},{6,0},{8,14},{10,12},{12,10},{14,8},{16,22},{18,... | collective-permute-start | bytes 718856 | tf_op jit(solution)/shard_map/ppermute | solution.py:673
  191.1 15.6 %collective-permute-start.28 = (bf16[3,48,576]{2,1,0:T(8,128)(2,1)S(1)}, bf16[3,48,576]{2,1,0:T(8,128)(2,1)S(1)}, u32[]{:S(2)}, u32[]{:S(2)}) collective-permute-start(bf16[3,48,576]{2,1,0:T(8,128)(2,1)S(1)} %get-tuple-element.129), channel_id=1, source_target_pairs={{0,16},{2,18},{4,20},{6,22},{8,24},{10,26},{12,28},{14,30},{16,0},... | collective-permute-start | bytes 497672 | tf_op jit(solution)/shard_map/ppermute | solution.py:673
  192.4 14.3 %collective-permute-start.29 = (bf16[3,48,576]{2,1,0:T(8,128)(2,1)S(1)}, bf16[3,48,576]{2,1,0:T(8,128)(2,1)S(1)}, u32[]{:S(2)}, u32[]{:S(2)}) collective-permute-start(bf16[3,48,576]{2,1,0:T(8,128)(2,1)S(1)} %get-tuple-element.130), channel_id=1, source_target_pairs={{0,24},{2,26},{4,28},{6,30},{8,16},{10,18},{12,20},{14,22},{16,8},... | collective-permute-start | bytes 497672 | tf_op jit(solution)/shard_map/ppermute | solution.py:673
  206.7 14.3 %collective-permute-start.34 = (bf16[2,576,512]{2,1,0:T(8,128)(2,1)}, bf16[2,576,512]{2,1,0:T(8,128)(2,1)S(1)}, u32[]{:S(2)}, u32[]{:S(2)}) collective-permute-start(bf16[2,576,512]{2,1,0:T(8,128)(2,1)} %get-tuple-element.138), channel_id=1, source_target_pairs={{0,1},{1,0},{2,3},{3,2},{4,5},{5,4},{6,7},{7,6},{8,9},{9,8},{10,11... | collective-permute-start | bytes 3538952 | tf_op jit(solution)/shard_map/ppermute | solution.py:677
  206.7 0.7 copy-start.7
  206.7 0.8 copy-start.12
  206.7 0.8 copy-start.13
  207.6 13.5 %collective-permute-start.33 = (bf16[2,576,512]{2,1,0:T(8,128)(2,1)}, bf16[2,576,512]{2,1,0:T(8,128)(2,1)S(1)}, u32[]{:S(2)}, u32[]{:S(2)}) collective-permute-start(bf16[2,576,512]{2,1,0:T(8,128)(2,1)} %get-tuple-element.137), channel_id=1, source_target_pairs={{0,1},{1,0},{2,3},{3,2},{4,5},{5,4},{6,7},{7,6},{8,9},{9,8},{10,11... | collective-permute-start | bytes 3538952 | tf_op jit(solution)/shard_map/ppermute | solution.py:677
  208.1 6.1 %copy-start.8 = (bf16[3,48,576]{2,1,0:T(8,128)(2,1)S(1)}, bf16[3,48,576]{2,1,0:T(8,128)(2,1)}, u32[]{:S(2)}) copy-start(bf16[3,48,576]{2,1,0:T(8,128)(2,1)} %copy-done.7) | copy-start | bytes 497668
  209.4 6.4 %collective-permute-start.32 = (bf16[64,576]{1,0:T(8,128)(2,1)S(1)}, bf16[64,576]{1,0:T(8,128)(2,1)S(1)}, u32[]{:S(2)}, u32[]{:S(2)}) collective-permute-start(bf16[64,576]{1,0:T(8,128)(2,1)S(1)} %concatenate.20), channel_id=1, source_target_pairs={{0,24},{2,26},{4,28},{6,30},{8,16},{10,18},{12,20},{14,22},{16,8},... | collective-permute-start | bytes 221192 | tf_op jit(solution)/shard_map/ppermute | solution.py:673
  210.9 6.5 %collective-permute-start.30 = (bf16[64,576]{1,0:T(8,128)(2,1)S(1)}, bf16[64,576]{1,0:T(8,128)(2,1)S(1)}, u32[]{:S(2)}, u32[]{:S(2)}) collective-permute-start(bf16[64,576]{1,0:T(8,128)(2,1)S(1)} %get-tuple-element.176), channel_id=1, source_target_pairs={{0,8},{2,10},{4,12},{6,14},{8,0},{10,2},{12,4},{14,6},{16,24},{18,... | collective-permute-start | bytes 221192 | tf_op jit(solution)/shard_map/ppermute | solution.py:673
  214.0 6.9 %collective-permute-start.31 = (bf16[64,576]{1,0:T(8,128)(2,1)S(1)}, bf16[64,576]{1,0:T(8,128)(2,1)S(1)}, u32[]{:S(2)}, u32[]{:S(2)}) collective-permute-start(bf16[64,576]{1,0:T(8,128)(2,1)S(1)} %get-tuple-element.177), channel_id=1, source_target_pairs={{0,16},{2,18},{4,20},{6,22},{8,24},{10,26},{12,28},{14,30},{16,0},... | collective-permute-start | bytes 221192 | tf_op jit(solution)/shard_map/ppermute | solution.py:673
  223.6 10.2 %all-to-all-start = ((f32[32,1,128]{2,1,0:T(1,128)}), f32[32,1,128]{2,1,0:T(1,128)S(1)}, u32[]{:S(2)}, u32[]{:S(2)}) async-start(f32[32,1,128]{2,1,0:T(1,128)} %broadcast_in_dim_broadcast_in_dim.3), calls=%async_computation | async-start | bytes 32768 | tf_op jit(solution)/shard_map/all_to_all | solution.py:711
  227.8 8.0 %copy-start.17 = (f32[2,576]{1,0:T(2,128)S(1)}, f32[2,576]{1,0:T(2,128)}, u32[]{:S(2)}) copy-start(f32[2,576]{1,0:T(2,128)} %gain_row_ref.1) | copy-start | bytes 13828
  227.8 9.3 %copy-start.4 = (f32[48,576]{1,0:T(8,128)S(1)}, f32[48,576]{1,0:T(8,128)}, u32[]{:S(2)}) copy-start(f32[48,576]{1,0:T(8,128)} %param.17) | copy-start | bytes 331780
  227.8 9.3 %copy-start.14 = (f32[48,576]{1,0:T(8,128)S(1)}, f32[48,576]{1,0:T(8,128)}, u32[]{:S(2)}) copy-start(f32[48,576]{1,0:T(8,128)} %param.18) | copy-start | bytes 331780
  227.8 9.3 %copy-start.15 = (f32[48,576]{1,0:T(8,128)S(1)}, f32[48,576]{1,0:T(8,128)}, u32[]{:S(2)}) copy-start(f32[48,576]{1,0:T(8,128)} %param.19) | copy-start | bytes 331780
  227.8 10.1 %copy-start.9 = (bf16[3,48,576]{2,1,0:T(8,128)(2,1)S(1)}, bf16[3,48,576]{2,1,0:T(8,128)(2,1)}, u32[]{:S(2)}) copy-start(bf16[3,48,576]{2,1,0:T(8,128)(2,1)} %copy-done.7) | copy-start | bytes 497668
  227.8 10.1 %copy-start.10 = (f32[3,48,576]{2,1,0:T(8,128)S(1)}, f32[3,48,576]{2,1,0:T(8,128)}, u32[]{:S(2)}) copy-start(f32[3,48,576]{2,1,0:T(8,128)} %param.21) | copy-start | bytes 995332
  227.9 10.1 %copy-start.11 = (f32[3,48,576]{2,1,0:T(8,128)S(1)}, f32[3,48,576]{2,1,0:T(8,128)}, u32[]{:S(2)}) copy-start(f32[3,48,576]{2,1,0:T(8,128)} %param.22) | copy-start | bytes 995332
where the time goes:
time: 243 us; the launch traced here: 241 us
  Pallas kernels  136 us (56%)
  starting transfers between devices  40.7 us (17%)
  waiting for transfers between devices  31.6 us (13%)
  other arithmetic  21.8 us (9%)
  local copies, waits for them, and re-layouts  5.36 us (2%)
  between operations  5.07 us (2%)
    pallas_call x1, Pallas kernels, feed_forward(): pl.pallas_call(functools.partial(feed_body, part_count), grid_spec=pltpu....  54.7 us
    pallas_call x1, Pallas kernels, attention_backward(): pl.pallas_call(attention_backward_body, grid_spec=pltpu.PrefetchScalarGri...  36 us
    ppermute x24, starting transfers between devices, partner(): return lax.ppermute(values, 'wide', [(i, i ^ mask) for i in range(count)])  35.3 us
    pallas_call x1, Pallas kernels, attention_forward(): pl.pallas_call(attention_forward_body, grid_spec=pltpu.PrefetchScalarGrid...  27.3 us
    ppermute x24, waiting for transfers between devices, partner(): return lax.ppermute(values, 'wide', [(i, i ^ mask) for i in range(count)])  20.7 us
    pallas_call x1, Pallas kernels, input_grads(): pl.pallas_call(input_grads_body, grid_spec=pltpu.PrefetchScalarGridSpec(n...  10.3 us
    pallas_call x1, Pallas kernels, branch_backward(): pl.pallas_call(branch_backward_body, grid=(2 * count,), in_specs=[step, s...  7.66 us
    ppermute x11, waiting for transfers between devices, across(): return lax.ppermute(values, 'narrow', [(0, 1), (1, 0)])  7.38 us
  transfers between devices with their start and end apart: 36, of which 15 were waited for; matrix products, arithmetic and copies ran while one was open for 6% of the time, Pallas kernels for 34%

commit v1 on v0

--- a/solution.py
+++ b/solution.py
@@ -118,6 +118,7 @@
     value_ref,
     mixed_ref,
     total_ref,
+    normed_ref,
     weight_ref,
     out_weight_ref,
     out_rows,
@@ -146,6 +147,7 @@
     normed = (x * inverse_root(x) * gain_ref[:, 0:1]).astype(BF16)
     cosine = cosine_ref[...]
     sine = sine_ref[...]
+    normed_ref[0] = normed
     projected = dot(weight_ref[...], normed)
     for head in range(HEADS):
         rows = slice(head * 64, head * 64 + 64)
@@ -221,6 +223,7 @@
         ((count, KV_WIDTH, length), BF16),
         ((count, D, length), BF16),
         ((count, KV_HEADS, 8, length), F32),
+        ((count, D, length), BF16),
     ]
     weights = (QKV, D), (D, D)
     return pl.pallas_call(
@@ -421,13 +424,11 @@
 
 def attention_backward_body(
     info_ref,
-    own_ref,
-    other_ref,
+    normed_ref,
     start_ref,
-    gain_ref,
     gain_row_ref,
-    weight_ref,
-    out_grad_ref,
+    weight_hbm,
+    out_grad_hbm,
     gain_second_ref,
     cosine_ref,
     sine_ref,
@@ -445,8 +446,21 @@
     grad_key,
     grad_value,
     weight_sums,
+    weight_ref,
+    out_grad_ref,
+    semaphores,
 ):
     step = pl.program_id(0)
+    copies = [
+        pltpu.make_async_copy(weight_hbm, weight_ref, semaphores.at[0]),
+        pltpu.make_async_copy(out_grad_hbm, out_grad_ref, semaphores.at[1]),
+    ]
+
+    @pl.when(step == 0)
+    def _():
+        for copy in copies:
+            copy.start()
+
     length = query_ref.shape[2]
     cosine = cosine_ref[...]
     sine = sine_ref[...]
@@ -517,9 +531,7 @@
         row += KV_WIDTH
         projected_ref[0, row : row + 64] = grad_value[member].astype(BF16)
 
-    x = joined(own_ref[0], other_ref[0], info_ref[0]).astype(F32)
-    normed = (x * inverse_root(x) * gain_ref[:, 0:1]).astype(BF16)
-    product = dot(projected_ref[0], normed, 1, 1)
+    product = dot(projected_ref[0], normed_ref[0], 1, 1)
 
     @pl.when(step == 0)
     def _():
@@ -531,6 +543,8 @@
 
     @pl.when(step == pl.num_programs(0) - 1)
     def _():
+        for copy in copies:
+            copy.wait()
         rows = 48
         pairs = (QKV + D) // (2 * rows)
         first = info_ref[0] == 0
@@ -561,26 +575,24 @@
 
 
 def attention_backward(
-    info, own, other, start, gain, gain_rows, weight, out_grad, gain_second, tables, parts, pieces
+    info, normed, start, gain_rows, weight, out_grad, gain_second, tables, parts, pieces
 ):
-    count = other.shape[0]
-    length = 2 * other.shape[2]
+    count, _, length = normed.shape
     held = (pieces, (QKV + D) // (2 * pieces) + 16, D)
     projected = (count, QKV, length)
-    fixed = [gain, gain_rows, weight, out_grad, gain_second, *tables]
+    before, after = [gain_rows], [gain_second, *tables]
     return pl.pallas_call(
         attention_backward_body,
         grid_spec=pltpu.PrefetchScalarGridSpec(
             num_scalar_prefetch=1,
             grid=(count,),
             in_specs=[
-                pl.BlockSpec(
-                    (1,) + own.shape[1:], lambda i, info: (info[0] * count + i, 0, 0)
-                ),
-                step_spec(other.shape),
+                step_spec(normed.shape),
                 step_spec(start.shape),
             ]
-            + [whole(part.shape) for part in fixed]
+            + [whole(part.shape) for part in before]
+            + [pl.BlockSpec(memory_space=pl.ANY)] * 2
+            + [whole(part.shape) for part in after]
             + [step_spec(part.shape) for part in parts],
             out_specs=[step_spec(projected)] + [whole(held)] * 2,
             scratch_shapes=[
@@ -589,6 +601,9 @@
                 pltpu.VMEM((KV_HEADS, HEAD_DIM, length), F32),
                 pltpu.VMEM((KV_HEADS, HEAD_DIM, length), F32),
                 pltpu.VMEM((QKV, D), F32),
+                pltpu.VMEM(weight.shape, BF16),
+                pltpu.VMEM(out_grad.shape, F32),
+                pltpu.SemaphoreType.DMA((2,)),
             ],
         ),
         out_shape=[jax.ShapeDtypeStruct(projected, BF16)]
@@ -598,7 +613,7 @@
             flops=9_000_000_000, transcendentals=6_000_000, bytes_accessed=15_000_000
         ),
         name="attention_backward",
-    )(info, own, other, start, *fixed, *parts)
+    )(info, normed, start, *before, weight, out_grad, *after, *parts)
 
 
 def input_grads_body(
@@ -705,14 +720,66 @@
     return (master_new, first_new, second_new)
 
 
-def to_all(row):
-    devices = lax.axis_size("wide") * lax.axis_size("narrow")
-    sent = jnp.broadcast_to(row, (devices, row.shape[1]))
-    return lax.all_to_all(sent, ("wide", "narrow"), 0, 0, tiled=True)
-
-
-def sum_everywhere(value):
-    return jnp.sum(to_all(jnp.full((1, 128), value, F32))[:, 0])
+def squares_body(count, rows, *refs):
+    attention_ref, gain_ref, feedforward_ref, sent_ref = refs[2 * count :]
+    attention = add_all([ref[...] for ref in refs[:count]])
+    feedforward = add_all([ref[...] for ref in refs[count : 2 * count]])
+    owned = attention[:rows]
+    attention_ref[...] = owned
+    if attention.shape[0] > rows:
+        gain_ref[...] = attention[rows : rows + 2]
+    else:
+        gain_ref[...] = jnp.zeros_like(gain_ref)
+    feedforward_ref[...] = feedforward
+    local = jnp.sum(owned * owned) + jnp.sum(feedforward * feedforward)
+    sent_ref[...] = jnp.full(sent_ref.shape, local, F32)
+
+
+def last_sums(attention, feedforward, rows, devices):
+    parts = attention + feedforward
+    shapes = [(rows, D), (2, D), feedforward[0].shape, (devices, 1, 128)]
+    return pl.pallas_call(
+        functools.partial(squares_body, len(attention), rows),
+        in_specs=[pl.BlockSpec(memory_space=pltpu.VMEM) for _ in parts],
+        out_specs=[pl.BlockSpec(memory_space=pltpu.VMEM) for _ in shapes],
+        out_shape=[jax.ShapeDtypeStruct(shape, F32) for shape in shapes],
+        cost_estimate=SHORT,
+        name="last_sums",
+    )(*parts)
+
+
+def update_body(squares_ref, *refs):
+    grads, states, results, norm_ref = refs[:3], refs[3:12], refs[12:21], refs[21]
+    gain_grad = grads[2][...]
+    squares = jnp.sum(squares_ref[...], axis=0)[:, 0:1] + jnp.sum(gain_grad * gain_grad)
+    norm = jnp.sqrt(squares)
+    norm_ref[...] = norm
+    factor = jnp.minimum(1.0, clip_limit / (norm + 1e-06))
+    rates = (rate_matrix, weight_decay), (rate_matrix, weight_decay), (rate_gain, 0.0)
+    for kind, (step_rate, decay_rate) in enumerate(rates):
+        grad = grads[kind][...]
+        scale = factor.reshape((1,) * grad.ndim)
+        new = adamw_update(
+            *[ref[...] for ref in states[3 * kind : 3 * kind + 3]],
+            grad,
+            scale,
+            step_rate,
+            decay_rate,
+        )
+        for ref, value in zip(results[3 * kind : 3 * kind + 3], new):
+            ref[...] = value
+
+
+def update(squares, grads, states):
+    shapes = [state.shape for state in states] + [(1, 1)]
+    return pl.pallas_call(
+        update_body,
+        in_specs=[pl.BlockSpec(memory_space=pltpu.VMEM) for _ in range(13)],
+        out_specs=[pl.BlockSpec(memory_space=pltpu.VMEM) for _ in shapes],
+        out_shape=[jax.ShapeDtypeStruct(shape, F32) for shape in shapes],
+        cost_estimate=SHORT,
+        name="update",
+    )(squares, *grads, *states)
 
 
 def per_device(
@@ -742,24 +809,21 @@
     cotangent_own = jnp.swapaxes(cotangent, 1, 2)
 
     def swap(tensor):
-        return across(jnp.where(first, tensor[own_count:], tensor[:own_count]))
+        return across(
+            lax.dynamic_slice_in_dim(tensor, (1 - place) * own_count, own_count, 0)
+        )
+
+    x_other = swap(x_own)
+    own_docs = lax.dynamic_slice_in_dim(documents, place * own_count, own_count, 0)
+    start = jnp.zeros_like(own_docs)
+    for number in (1, 2):
+        before = jnp.sum((own_docs < number).astype(jnp.int32), axis=1, keepdims=True)
+        start = jnp.where(own_docs == number, before, start)
+    start = start[:, None, :]
 
     rows = attention_master.shape[0]
     aligned = rows % 16 == 0
-    piece = attention_master.astype(BF16)
-    parts = [piece] + [partner(piece, k * inner) for k in range(1, outer)]
-    stack = jnp.stack(parts if aligned else in_order(parts, outer_place))
-    parts = [stack] + [partner(stack, k) for k in range(1, inner)]
-    feed_piece = feedforward_master.astype(BF16)
-    feed_outer = jnp.stack(
-        [feed_piece] + [partner(feed_piece, k * inner) for k in range(1, outer)]
-    )
-    feed_outer, parts[1:] = lax.optimization_barrier((feed_outer, parts[1:]))
-    feed_parts = [feed_outer] + [partner(feed_outer, k) for k in range(1, inner)]
     if aligned:
-        stack = jnp.stack(parts)
-        pieces_own = stack.reshape(-1, rows, D)
-        pieces_other = across(stack).reshape(-1, rows, D)
         chunk = jnp.arange(2 * inner * outer, dtype=jnp.int32)
         order = (
             ((chunk % 2) ^ place) * inner + ((chunk // 2 % inner) ^ inner_place)
@@ -769,9 +833,6 @@
         row_of = ((pair // inner) ^ outer_place) * rows
         grad_pieces = inner
     else:
-        stack = jnp.stack(in_order(parts, inner_place), axis=1)
-        pieces = jnp.stack(in_order([stack, across(stack)], place), axis=2).reshape(-1, 48, D)
-        pieces_own, pieces_other = pieces[:16], pieces[16:]
         order = jnp.arange(32, dtype=jnp.int32)
         piece_of = jnp.zeros((16,), jnp.int32)
         row_of = jnp.arange(16, dtype=jnp.int32) * 48
@@ -780,17 +841,29 @@
         [jnp.full((1,), place), order, piece_of, row_of]
     ).astype(jnp.int32)
 
-    x_other = swap(x_own)
-    own_docs = lax.dynamic_slice_in_dim(documents, place * own_count, own_count, 0)
-    start = jnp.zeros_like(own_docs)
-    for number in (1, 2):
-        before = jnp.sum((own_docs < number).astype(jnp.int32), axis=1, keepdims=True)
-        start = jnp.where(own_docs == number, before, start)
-    start = start[:, None, :]
-
+    piece = attention_master.astype(BF16)
+    parts = [piece] + [partner(piece, k * inner) for k in range(1, outer)]
+    stack = jnp.stack(parts if aligned else in_order(parts, outer_place))
+    feed_piece = feedforward_master.astype(BF16)
+    feed_outer = jnp.stack(
+        [feed_piece] + [partner(feed_piece, k * inner) for k in range(1, outer)]
+    )
+    parts = [stack] + [partner(stack, k) for k in range(1, inner)]
+    feed_outer, parts[1:], info, start, gain_columns = lax.optimization_barrier(
+        (feed_outer, parts[1:], info, start, gain_columns)
+    )
+    feed_parts = [feed_outer] + [partner(feed_outer, k) for k in range(1, inner)]
+    if aligned:
+        stack = jnp.stack(parts)
+        pieces_own = stack.reshape(-1, rows, D)
+        pieces_other = across(stack).reshape(-1, rows, D)
+    else:
+        stack = jnp.stack(in_order(parts, inner_place), axis=1)
+        pieces = jnp.stack(in_order([stack, across(stack)], place), axis=2).reshape(-1, 48, D)
+        pieces_own, pieces_other = pieces[:16], pieces[16:]
     cotangent_other = swap(cotangent_own)
 
-    residual, query, key, value, mixed, total, weight_qkv, weight_out = attention_forward(
+    residual, query, key, value, mixed, total, normed, weight_qkv, weight_out = attention_forward(
         info, x_own, x_other, start, pieces_own, pieces_other, gain_columns, tables
     )
     feed_parts, residual = lax.optimization_barrier((feed_parts, residual))
@@ -821,10 +894,8 @@
     feed_got = [feed_sums[0]] + [partner(feed_sums[k], k) for k in range(1, inner)]
     projected, kept, sent = attention_backward(
         info,
-        x_own,
-        x_other,
+        normed,
         start,
-        gain_columns,
         gain_master,
         weight_qkv,
         out_grad,
@@ -861,46 +932,35 @@
         ]
     else:
         parts = in_order([total[k] for k in range(outer)], outer_place)
-    attention_grad = add_all(
-        [parts[0]] + [partner(parts[k], k * inner) for k in range(1, outer)]
+    last = [parts[0]] + [partner(parts[k], k * inner) for k in range(1, outer)]
+    devices = lax.axis_size("wide") * lax.axis_size("narrow")
+    attention_grad, gain_total, feedforward_grad, squares = last_sums(
+        last, feed_last, rows, devices
     )
     if aligned:
-        attention_grad, gain_grad = attention_grad[:rows], attention_grad[rows : rows + 2]
-    feedforward_grad = add_all(feed_last)
+        gain_grad = gain_total
+    squares = lax.all_to_all(squares, ("wide", "narrow"), 0, 0, tiled=True)
     grad_received = across(grad_other)
     attention_grad, gain_grad, grad_received, out_received = lax.optimization_barrier(
         (attention_grad, gain_grad, grad_received, out_received)
     )
     grad_tokens = place_other(grad_own, grad_received)
     outputs = place_other(outputs, out_received)
-    local_squares = jnp.sum(attention_grad * attention_grad) + jnp.sum(
-        feedforward_grad * feedforward_grad
-    )
-    grad_norm = jnp.sqrt(sum_everywhere(local_squares) + jnp.sum(gain_grad * gain_grad))
-    factor = jnp.minimum(1.0, clip_limit / (grad_norm + 1e-06))
-    update = functools.partial(adamw_update, factor=factor)
-    attention_new = update(
+    states = (
         attention_master,
         attention_first,
         attention_second,
-        attention_grad,
-        step_rate=rate_matrix,
-        decay_rate=weight_decay,
-    )
-    feedforward_new = update(
         feedforward_master,
         feedforward_first,
         feedforward_second,
-        feedforward_grad,
-        step_rate=rate_matrix,
-        decay_rate=weight_decay,
-    )
-    gain_new = update(
-        gain_master, gain_first, gain_second, gain_grad, step_rate=rate_gain, decay_rate=0.0
-    )
+        gain_master,
+        gain_first,
+        gain_second,
+    )
+    *updated, grad_norm = update(squares, (attention_grad, feedforward_grad, gain_grad), states)
     outputs = jnp.swapaxes(outputs, 1, 2)
     grad_tokens = jnp.swapaxes(grad_tokens, 1, 2)
-    return (outputs, grad_tokens, grad_norm, *attention_new, *feedforward_new, *gain_new)
+    return (outputs, grad_tokens, grad_norm.reshape(()), *updated)
 
 
 def solution(mesh):

time: 243 us -> 238 us (0.979)
  other arithmetic: 21.8 us -> 15.6 us
  Pallas kernels: 136 us -> 140 us
  between operations: 5.07 us -> 1.29 us
  waiting for transfers between devices: 31.6 us -> 27.9 us
  local copies, waits for them, and re-layouts: 5.36 us -> 8.75 us
    pallas_call x0 -> x2, Pallas kernels: none -> 5.62 us  [the longest x1 3.28 us: update(): pl.pallas_call(update_body, in_specs=[pl.BlockSpec(memory_space=pltpu.VME...]
    ppermute x24, waiting for transfers between devices: 20.7 us -> 16.3 us  [partner(): return lax.ppermute(values, 'wide', [(i, i ^ mask) for i in range(count)])]
    select_n x2 -> x0, other arithmetic: 3.98 us -> none  [swap(): return across(jnp.where(first, tensor[own_count:], tensor[:own_count]))]
    sub x3 -> x0, other arithmetic: 3.34 us -> none  [adamw_update(): master * (1.0 - step_rate * decay_rate)]
    another operation x2, other arithmetic: 0.17 us -> 3.27 us  [per_device(): jnp.stack([feed_piece] + [partner(feed_piece, k * inner) for k in range(1...]
    reduce_sum x4 -> x0, other arithmetic: 2.55 us -> none  [the longest x1 0.72 us: per_device(): jnp.sum(feedforward_grad * feedforward_grad)]
  transfers between devices with their start and end apart: 36 -> 36, of which waited for: 15 -> 12; matrix products, arithmetic and copies ran while one was open for 6% -> 6% of each run, Pallas kernels for 34% -> 35%
where the time goes in v1:
time: 238 us; the launch traced here: 235 us
  Pallas kernels  140 us (59%)
  starting transfers between devices  41.4 us (17%)
  waiting for transfers between devices  27.9 us (12%)
  other arithmetic  15.6 us (7%)
  local copies, waits for them, and re-layouts  8.75 us (4%)
    pallas_call x1, Pallas kernels, feed_forward(): pl.pallas_call(functools.partial(feed_body, part_count), grid_spec=pltpu....  54.7 us
    ppermute x24, starting transfers between devices, partner(): return lax.ppermute(values, 'wide', [(i, i ^ mask) for i in range(count)])  35.8 us
    pallas_call x1, Pallas kernels, attention_backward(): pl.pallas_call(attention_backward_body, grid_spec=pltpu.PrefetchScalarGri...  33.9 us
    pallas_call x1, Pallas kernels, attention_forward(): pl.pallas_call(attention_forward_body, grid_spec=pltpu.PrefetchScalarGrid...  28.2 us
    ppermute x24, waiting for transfers between devices, partner(): return lax.ppermute(values, 'wide', [(i, i ^ mask) for i in range(count)])  16.3 us
    pallas_call x1, Pallas kernels, input_grads(): pl.pallas_call(input_grads_body, grid_spec=pltpu.PrefetchScalarGridSpec(n...  10.4 us
    pallas_call x1, Pallas kernels, branch_backward(): pl.pallas_call(branch_backward_body, grid=(2 * count,), in_specs=[step, s...  7.61 us
    ppermute x11, waiting for transfers between devices, across(): return lax.ppermute(values, 'narrow', [(0, 1), (1, 0)])  7.25 us
  transfers between devices with their start and end apart: 36, of which 12 were waited for; matrix products, arithmetic and copies ran while one was open for 6% of the time, Pallas kernels for 35%

profile of v1, /device:TPU:0, one launch (start us, length us, event | category | flops | bytes accessed | tf_op | source)
XLA Modules:
  0.0 235.4 jit_solution(3751082931726861798)
XLA Ops:
  0.7 0.9 convert_element_type.158
  1.6 4.1 %collective-permute-start.4 = (bf16[48,576]{1,0:T(8,128)(2,1)S(1)}, bf16[48,576]{1,0:T(8,128)(2,1)S(1)}, u32[]{:S(2)}, u32[]{:S(2)}) collective-permute-start(bf16[48,576]{1,0:T(8,128)(2,1)S(1)} %convert_element_type.158), channel_id=1, source_target_pairs={{0,16},{2,18},{4,20},{6,22},{8,24},{10,26},{12,28},{14,30},{16,0},... | collective-permute-start | bytes 165896 | tf_op jit(solution)/shard_map/ppermute | solution.py:688
  5.7 1.6 collective-permute-start.3
  7.2 1.7 convert_element_type.157
  8.9 1.9 collective-permute-start.1
  10.8 2.5 %collective-permute-start = (bf16[3,48,576]{2,1,0:T(8,128)(2,1)}, bf16[3,48,576]{2,1,0:T(8,128)(2,1)}, u32[]{:S(2)}, u32[]{:S(2)}) collective-permute-start(bf16[3,48,576]{2,1,0:T(8,128)(2,1)} %convert_element_type.157), channel_id=1, source_target_pairs={{0,8},{2,10},{4,12},{6,14},{8,0},{10,2},{12,4},{14,6},{16,24},{18,... | collective-permute-start | bytes 497672 | tf_op jit(solution)/shard_map/ppermute | solution.py:688
  13.3 0.9 convert_bitcast_fusion
  14.2 1.0 convert_bitcast_fusion.1
  15.5 1.4 dynamic-slice_bitcast_fusion.1
  17.2 2.6 %collective-permute-start.8 = (bf16[4,48,576]{2,1,0:T(8,128)(2,1)S(1)}, bf16[4,48,576]{2,1,0:T(8,128)(2,1)S(1)}, u32[]{:S(2)}, u32[]{:S(2)}) collective-permute-start(bf16[4,48,576]{2,1,0:T(8,128)(2,1)S(1)} %get-tuple-element.202), channel_id=1, source_target_pairs={{0,6},{2,4},{4,2},{6,0},{8,14},{10,12},{12,10},{14,8},{16,22},{18,... | collective-permute-start | bytes 663560 | tf_op jit(solution)/shard_map/ppermute | solution.py:688
  19.8 5.6 %collective-permute-done.1 = bf16[3,48,576]{2,1,0:T(8,128)(2,1)} collective-permute-done((bf16[3,48,576]{2,1,0:T(8,128)(2,1)}, bf16[3,48,576]{2,1,0:T(8,128)(2,1)}, u32[]{:S(2)}, u32[]{:S(2)}) %collective-permute-start.1) | collective-permute-done | bytes 165920 | tf_op jit(solution)/shard_map/ppermute | solution.py:688
  25.4 1.5 collective-permute-start.7
  27.0 1.5 collective-permute-start.6
  28.4 0.6 pad_add_fusion.info_ref
  29.0 0.6 broadcast_in_dim.28.start_ref
  29.6 0.9 copy.27
  30.5 2.3 pad_maximum_fusion.1.refs_0_
  32.8 0.5 collective-permute-done.6
  33.3 1.1 pad_maximum_fusion
  34.6 0.5 collective-permute-start.14
  35.1 1.4 collective-permute-start.11
  36.6 1.5 collective-permute-start.10
  38.1 0.5 collective-permute-start.9
  39.1 0.6 copy-done.1
  39.7 28.2 %attention_forward.1 = (f32[2,576,1024]{2,1,0:T(8,128)}, bf16[2,576,1024]{2,1,0:T(8,128)(2,1)}, bf16[2,192,1024]{2,1,0:T(8,128)(2,1)}, bf16[2,192,1024]{2,1,0:T(...) custom-call(s32[65]{0:T(128)} %pad_add_fusion.info_ref, ...), custom_call_target="tpu_custom_call" | custom-call | flops 8000000000 | bytes 20000000 | tf_op jit(solution)/shard_map/attention_forward/pallas_call | solution.py:229
  67.9 2.7 %collective-permute-done.10.refs_2_ = bf16[4,3,48,576]{3,2,1,0:T(8,128)(2,1)} collective-permute-done((bf16[4,3,48,576]{3,2,1,0:T(8,128)(2,1)}, bf16[4,3,48,576]{3,2,1,0:T(8,128)(2,1)}, u32[]{:S(2)}, u32[]{:S(2)}) %collective-permute-start.10) | collective-permute-done | bytes 663584 | tf_op jit(solution)/shard_map/ppermute | solution.py:688
  70.6 0.5 collective-permute-start.16
  71.2 0.5 collective-permute-start.18
  71.7 1.4 collective-permute-done.15.refs_4_
  73.1 2.1 collective-permute-done.16.refs_5_
  75.2 1.1 collective-permute-done.17.refs_6_
  76.2 0.8 copy-done.18
  77.1 54.7 %feed_forward.1 = (bf16[4,576,512]{2,1,0:T(8,128)(2,1)}, bf16[2,576,512]{2,1,0:T(8,128)(2,1)}, bf16[2,576,1024]{2,1,0:T(8,128)(2,1)}, f32[1,576]{1,0:T(1,128)}, ...) custom-call(s32[65]{0:T(128)} %pad_add_fusion.info_ref, ...), custom_call_target="tpu_custom_call" | custom-call | flops 32000000000 | bytes 30000000 | tf_op jit(solution)/shard_map/feed_forward/pallas_call | solution.py:352
  132.0 7.6 %branch_backward.1 = (bf16[2,576,1024]{2,1,0:T(8,128)(2,1)}, f32[2,3,8,1024]{3,2,1,0:T(8,128)}, f32[576,576]{1,0:T(8,128)}) custom-call(bf16[2,576,1024]{2,1,0:T(8,128)(2,1)} %get-tuple-element.114.grad_ref, bf16[2,576,1024]{2,1,0:T(8,128)(2,1)} %get-tuple-element.115.mixed_ref, bf16[576,576]{1,0:T(8,128)(2,1)} %get-tuple-element.116.weight_ref), custom_call_target="tpu_custom_call" | custom-call | flops 1000000 | bytes 100000 | tf_op jit(solution)/shard_map/branch_backward/pallas_call | solution.py:405
  139.6 3.6 %fusion.3 = (bf16[3,192,576]{2,1,0:T(8,128)(2,1)}, bf16[3,192,576]{2,1,0:T(8,128)(2,1)}, bf16[3,192,576]{2,1,0:T(8,128)(2,1)}, bf16[3,192,576]{2,1,0:T(8,128)(2,1)S(1)}) fusion(bf16[4,3,192,576]{3,2,1,0:T(8,128)(2,1)} %collective-permute-done.19, bf16[4,3,192,576]{3,2,1,0:T(8,128)(2,1)S(1)} %copy-done), kind=kLoop, calls=%fused_computation.12 | loop fusion | flops 5308416 | bytes 7962624 | tf_op jit(solution)/shard_map/convert_element_type | solution.py:892
  143.3 0.8 collective-permute-start.20
  144.1 1.3 collective-permute-start.21
  145.4 1.4 collective-permute-start.22
  146.8 33.9 %attention_backward.1 = (bf16[2,960,1024]{2,1,0:T(8,128)(2,1)}, bf16[4,208,576]{2,1,0:T(8,128)(2,1)}, bf16[4,208,576]{2,1,0:T(8,128)(2,1)}) custom-call(s32[65]{0:T(128)} %pad_add_fusion.info_ref, bf16[2,576,1024]{2,1,0:T(8,128)(2,1)} %get-tuple-element.125.normed_ref, s32[2,1,1024]{2,1,0:T(1,128)} %broadcast_in_dim.28.start_ref, f32[2,576]{1,0:T(2,128)} %refs_9_.1, ...), custom_call_target="tpu_custom_call" | custom-call | flops 8999999488 | bytes 15000000 | tf_op jit(solution)/shard_map/attention_backward/pallas_call | solution.py:584
  181.1 0.7 slice_bitcast_fusion
  181.9 2.7 %collective-permute-done.23 = bf16[4,208,576]{2,1,0:T(8,128)(2,1)S(1)} collective-permute-done((bf16[4,208,576]{2,1,0:T(8,128)(2,1)S(1)}, bf16[4,208,576]{2,1,0:T(8,128)(2,1)S(1)}, u32[]{:S(2)}, u32[]{:S(2)}) %collective-permute-start.23) | collective-permute-done | bytes 958496 | tf_op jit(solution)/shard_map/ppermute | solution.py:692
  184.9 0.8 collective-permute-start.24
  185.7 1.3 collective-permute-start.25
  187.0 1.4 collective-permute-start.26
  188.4 0.6 collective-permute-start.28
  189.0 2.7 %collective-permute-start.29 = (bf16[3,48,576]{2,1,0:T(8,128)(2,1)S(1)}, bf16[3,48,576]{2,1,0:T(8,128)(2,1)S(1)}, u32[]{:S(2)}, u32[]{:S(2)}) collective-permute-start(bf16[3,48,576]{2,1,0:T(8,128)(2,1)S(1)} %get-tuple-element.152), channel_id=1, source_target_pairs={{0,24},{2,26},{4,28},{6,30},{8,16},{10,18},{12,20},{14,22},{16,8},... | collective-permute-start | bytes 497672 | tf_op jit(solution)/shard_map/ppermute | solution.py:688
  191.7 10.4 %input_grads.1 = (f32[4,576,512]{2,1,0:T(8,128)}, bf16[2,576,512]{2,1,0:T(8,128)(2,1)}) custom-call(s32[65]{0:T(128)} %pad_add_fusion.info_ref, bf16[4,576,512]{2,1,0:T(8,128)(2,1)} %bitcast.62, bf16[2,576,512]{2,1,0:T(8,128)(2,1)} %copy-done.1, f32[576,2]{1,0:T(8,128)} %bitcast.66, bf16[2,960,1024]{2,1,0:T(8,128)(2,1)} %get-tuple-element.153.projected_ref, ...), custom_call_target="tpu_custom_call" | custom-call | flops 1000000 | bytes 100000 | tf_op jit(solution)/shard_map/input_grads/pallas_call | solution.py:656
  202.0 1.2 collective-permute-done.28.refs_6_
  203.3 0.7 copy-done.7
  204.0 0.5 collective-permute-start.33
  204.6 0.7 pad_maximum_fusion.3
  205.3 4.0 %collective-permute-start.31 = (bf16[64,576]{1,0:T(8,128)(2,1)S(1)}, bf16[64,576]{1,0:T(8,128)(2,1)S(1)}, u32[]{:S(2)}, u32[]{:S(2)}) collective-permute-start(bf16[64,576]{1,0:T(8,128)(2,1)S(1)} %get-tuple-element.203), channel_id=1, source_target_pairs={{0,16},{2,18},{4,20},{6,22},{8,24},{10,26},{12,28},{14,30},{16,0},... | collective-permute-start | bytes 221192 | tf_op jit(solution)/shard_map/ppermute | solution.py:688
  209.3 2.2 collective-permute-start.32
  211.5 0.9 collective-permute-done.31.refs_2_
  212.4 1.7 collective-permute-done.30.refs_1_
  214.1 3.7 %collective-permute-done.32.refs_3_ = bf16[64,576]{1,0:T(8,128)(2,1)S(1)} collective-permute-done((bf16[64,576]{1,0:T(8,128)(2,1)S(1)}, bf16[64,576]{1,0:T(8,128)(2,1)S(1)}, u32[]{:S(2)}, u32[]{:S(2)}) %collective-permute-start.32) | collective-permute-done | bytes 73760 | tf_op jit(solution)/shard_map/ppermute | solution.py:688
  217.9 0.6 copy-done.10
  218.5 2.3 last_sums.1
  220.8 3.3 %all-to-all-start = ((f32[32,1,128]{2,1,0:T(1,128)}), f32[32,1,128]{2,1,0:T(1,128)S(1)}, u32[]{:S(2)}, u32[]{:S(2)}) async-start(f32[32,1,128]{2,1,0:T(1,128)} %get-tuple-element.170), calls=%async_computation | async-start | bytes 32768 | tf_op jit(solution)/shard_map/all_to_all | solution.py:942
  224.1 1.7 convert_dynamic-update-slice_fusion
  225.9 1.1 constant_dynamic-update-slice_fusion
  227.0 4.3 %all-to-all-done.squares_ref = f32[32,1,128]{2,1,0:T(1,128)S(1)} async-done(((f32[32,1,128]{2,1,0:T(1,128)}), f32[32,1,128]{2,1,0:T(1,128)S(1)}, u32[]{:S(2)}, u32[]{:S(2)}) %all-to-all-start) | async-done | bytes 16416 | tf_op jit(solution)/shard_map/all_to_all | solution.py:942
  231.3 0.6 copy-done.11
  231.8 3.3 %update.1 = (f32[48,576]{1,0:T(8,128)}, f32[48,576]{1,0:T(8,128)}, f32[48,576]{1,0:T(8,128)}, f32[3,48,576]{2,1,0:T(8,128)}, f32[3,48,576]{2,1,0:T(8,128)}, /*in...) custom-call(f32[32,1,128]{2,1,0:T(1,128)} %copy-done.11, ...), custom_call_target="tpu_custom_call" | custom-call | flops 1000000 | bytes 100000 | tf_op jit(solution)/shard_map/update/pallas_call | solution.py:775
  (81 shorter events, 2.3 us)
Async XLA Ops:
  0.6 14.6 %copy-start.13 = (s32[4,1024]{1,0:T(4,128)S(1)}, s32[4,1024]{1,0:T(4,128)}, u32[]{:S(2)}) copy-start(s32[4,1024]{1,0:T(4,128)} %param.16) | copy-start | bytes 49156
  1.6 15.4 %collective-permute-start.4 = (bf16[48,576]{1,0:T(8,128)(2,1)S(1)}, bf16[48,576]{1,0:T(8,128)(2,1)S(1)}, u32[]{:S(2)}, u32[]{:S(2)}) collective-permute-start(bf16[48,576]{1,0:T(8,128)(2,1)S(1)} %convert_element_type.158), channel_id=1, source_target_pairs={{0,16},{2,18},{4,20},{6,22},{8,24},{10,26},{12,28},{14,30},{16,0},... | collective-permute-start | bytes 165896 | tf_op jit(solution)/shard_map/ppermute | solution.py:688
  5.7 11.4 %collective-permute-start.3 = (bf16[48,576]{1,0:T(8,128)(2,1)S(1)}, bf16[48,576]{1,0:T(8,128)(2,1)S(1)}, u32[]{:S(2)}, u32[]{:S(2)}) collective-permute-start(bf16[48,576]{1,0:T(8,128)(2,1)S(1)} %convert_element_type.158), channel_id=1, source_target_pairs={{0,8},{2,10},{4,12},{6,14},{8,0},{10,2},{12,4},{14,6},{16,24},{18,... | collective-permute-start | bytes 165896 | tf_op jit(solution)/shard_map/ppermute | solution.py:688
  7.2 9.9 %collective-permute-start.5 = (bf16[48,576]{1,0:T(8,128)(2,1)S(1)}, bf16[48,576]{1,0:T(8,128)(2,1)S(1)}, u32[]{:S(2)}, u32[]{:S(2)}) collective-permute-start(bf16[48,576]{1,0:T(8,128)(2,1)S(1)} %convert_element_type.158), channel_id=1, source_target_pairs={{0,24},{2,26},{4,28},{6,30},{8,16},{10,18},{12,20},{14,22},{16,8},... | collective-permute-start | bytes 165896 | tf_op jit(solution)/shard_map/ppermute | solution.py:688
  8.9 16.5 %collective-permute-start.1 = (bf16[3,48,576]{2,1,0:T(8,128)(2,1)}, bf16[3,48,576]{2,1,0:T(8,128)(2,1)}, u32[]{:S(2)}, u32[]{:S(2)}) collective-permute-start(bf16[3,48,576]{2,1,0:T(8,128)(2,1)} %convert_element_type.157), channel_id=1, source_target_pairs={{0,16},{2,18},{4,20},{6,22},{8,24},{10,26},{12,28},{14,30},{16,0},... | collective-permute-start | bytes 497672 | tf_op jit(solution)/shard_map/ppermute | solution.py:688
  10.8 16.1 %collective-permute-start = (bf16[3,48,576]{2,1,0:T(8,128)(2,1)}, bf16[3,48,576]{2,1,0:T(8,128)(2,1)}, u32[]{:S(2)}, u32[]{:S(2)}) collective-permute-start(bf16[3,48,576]{2,1,0:T(8,128)(2,1)} %convert_element_type.157), channel_id=1, source_target_pairs={{0,8},{2,10},{4,12},{6,14},{8,0},{10,2},{12,4},{14,6},{16,24},{18,... | collective-permute-start | bytes 497672 | tf_op jit(solution)/shard_map/ppermute | solution.py:688
  15.5 14.1 %copy-start.12 = (f32[2,576]{1,0:T(2,128)S(1)}, f32[2,576]{1,0:T(2,128)}, u32[]{:S(2)}) copy-start(f32[2,576]{1,0:T(2,128)} %refs_9_.1) | copy-start | bytes 13828
  16.9 13.6 %collective-permute-start.2 = (bf16[3,48,576]{2,1,0:T(8,128)(2,1)}, bf16[3,48,576]{2,1,0:T(8,128)(2,1)}, u32[]{:S(2)}, u32[]{:S(2)}) collective-permute-start(bf16[3,48,576]{2,1,0:T(8,128)(2,1)} %convert_element_type.157), channel_id=1, source_target_pairs={{0,24},{2,26},{4,28},{6,30},{8,16},{10,18},{12,20},{14,22},{16,8},... | collective-permute-start | bytes 497672 | tf_op jit(solution)/shard_map/ppermute | solution.py:688
  17.0 21.6 %collective-permute-start.12 = (bf16[2,576,512]{2,1,0:T(8,128)(2,1)S(1)}, bf16[2,576,512]{2,1,0:T(8,128)(2,1)S(1)}, u32[]{:S(2)}, u32[]{:S(2)}) collective-permute-start(bf16[2,576,512]{2,1,0:T(8,128)(2,1)S(1)} %dynamic-slice_bitcast_fusion.1), channel_id=1, source_target_pairs={{0,1},{1,0},{2,3},{3,2},{4,5},{5,4},{6,7},{7,6},{8,9},{9,8},{10,11... | collective-permute-start | bytes 3538952 | tf_op jit(solution)/shard_map/ppermute | solution.py:692
  17.2 15.6 %collective-permute-start.8 = (bf16[4,48,576]{2,1,0:T(8,128)(2,1)S(1)}, bf16[4,48,576]{2,1,0:T(8,128)(2,1)S(1)}, u32[]{:S(2)}, u32[]{:S(2)}) collective-permute-start(bf16[4,48,576]{2,1,0:T(8,128)(2,1)S(1)} %get-tuple-element.202), channel_id=1, source_target_pairs={{0,6},{2,4},{4,2},{6,0},{8,14},{10,12},{12,10},{14,8},{16,22},{18,... | collective-permute-start | bytes 663560 | tf_op jit(solution)/shard_map/ppermute | solution.py:688
  25.4 7.4 %collective-permute-start.7 = (bf16[4,48,576]{2,1,0:T(8,128)(2,1)S(1)}, bf16[4,48,576]{2,1,0:T(8,128)(2,1)S(1)}, u32[]{:S(2)}, u32[]{:S(2)}) collective-permute-start(bf16[4,48,576]{2,1,0:T(8,128)(2,1)S(1)} %get-tuple-element.202), channel_id=1, source_target_pairs={{0,4},{2,6},{4,0},{6,2},{8,12},{10,14},{12,8},{14,10},{16,20},{18,... | collective-permute-start | bytes 663560 | tf_op jit(solution)/shard_map/ppermute | solution.py:688
  27.0 6.3 %collective-permute-start.6 = (bf16[4,48,576]{2,1,0:T(8,128)(2,1)S(1)}, bf16[4,48,576]{2,1,0:T(8,128)(2,1)}, u32[]{:S(2)}, u32[]{:S(2)}) collective-permute-start(bf16[4,48,576]{2,1,0:T(8,128)(2,1)S(1)} %get-tuple-element.202), channel_id=1, source_target_pairs={{0,2},{2,0},{4,6},{6,4},{8,10},{10,8},{12,14},{14,12},{16,18},{18,... | collective-permute-start | bytes 663560 | tf_op jit(solution)/shard_map/ppermute | solution.py:688
  30.5 4.0 %copy-start.4 = (bf16[4,512,576]{1,2,0:T(8,128)(2,1)S(1)}, bf16[4,512,576]{1,2,0:T(8,128)(2,1)}, u32[]{:S(2)}) copy-start(bf16[4,512,576]{1,2,0:T(8,128)(2,1)} %param.15) | copy-start | bytes 7077892
  34.4 4.2 %copy-start.3 = (bf16[4,4,48,576]{3,2,1,0:T(8,128)(2,1)}, bf16[4,4,48,576]{3,2,1,0:T(8,128)(2,1)S(1)}, u32[]{:S(2)}) copy-start(bf16[4,4,48,576]{3,2,1,0:T(8,128)(2,1)S(1)} %pad_maximum_fusion) | copy-start | bytes 2654212
  34.4 3.7 %collective-permute-start.13 = (bf16[4,4,48,576]{3,2,1,0:T(8,128)(2,1)S(1)}, bf16[4,4,48,576]{3,2,1,0:T(8,128)(2,1)S(1)}, u32[]{:S(2)}, u32[]{:S(2)}) collective-permute-start(bf16[4,4,48,576]{3,2,1,0:T(8,128)(2,1)S(1)} %pad_maximum_fusion), channel_id=1, source_target_pairs={{0,1},{1,0},{2,3},{3,2},{4,5},{5,4},{6,7},{7,6},{8,9},{9,8},{10,11... | collective-permute-start | bytes 2654216 | tf_op jit(solution)/shard_map/ppermute | solution.py:692
  34.6 37.1 %collective-permute-start.14 = (bf16[2,576,512]{2,1,0:T(8,128)(2,1)S(1)}, bf16[2,576,512]{2,1,0:T(8,128)(2,1)}, u32[]{:S(2)}, u32[]{:S(2)}) collective-permute-start(bf16[2,576,512]{2,1,0:T(8,128)(2,1)S(1)} %dynamic-slice_bitcast_fusion), channel_id=1, source_target_pairs={{0,1},{1,0},{2,3},{3,2},{4,5},{5,4},{6,7},{7,6},{8,9},{9,8},{10,11... | collective-permute-start | bytes 3538952 | tf_op jit(solution)/shard_map/ppermute | solution.py:692
  35.1 32.8 %collective-permute-start.11 = (bf16[4,3,48,576]{3,2,1,0:T(8,128)(2,1)}, bf16[4,3,48,576]{3,2,1,0:T(8,128)(2,1)}, u32[]{:S(2)}, u32[]{:S(2)}) collective-permute-start(bf16[4,3,48,576]{3,2,1,0:T(8,128)(2,1)} %pad_maximum_fusion.1.refs_0_), channel_id=1, source_target_pairs={{0,6},{2,4},{4,2},{6,0},{8,14},{10,12},{12,10},{14,8},{16,22},{18,... | collective-permute-start | bytes 1990664 | tf_op jit(solution)/shard_map/ppermute | solution.py:688
  36.6 34.1 %collective-permute-start.10 = (bf16[4,3,48,576]{3,2,1,0:T(8,128)(2,1)}, bf16[4,3,48,576]{3,2,1,0:T(8,128)(2,1)}, u32[]{:S(2)}, u32[]{:S(2)}) collective-permute-start(bf16[4,3,48,576]{3,2,1,0:T(8,128)(2,1)} %pad_maximum_fusion.1.refs_0_), channel_id=1, source_target_pairs={{0,4},{2,6},{4,0},{6,2},{8,12},{10,14},{12,8},{14,10},{16,20},{18,... | collective-permute-start | bytes 1990664 | tf_op jit(solution)/shard_map/ppermute | solution.py:688
  38.1 1.0 copy-start.15
  38.1 32.5 %collective-permute-start.9 = (bf16[4,3,48,576]{3,2,1,0:T(8,128)(2,1)}, bf16[4,3,48,576]{3,2,1,0:T(8,128)(2,1)}, u32[]{:S(2)}, u32[]{:S(2)}) collective-permute-start(bf16[4,3,48,576]{3,2,1,0:T(8,128)(2,1)} %pad_maximum_fusion.1.refs_0_), channel_id=1, source_target_pairs={{0,2},{2,0},{4,6},{6,4},{8,10},{10,8},{12,14},{14,12},{16,18},{18,... | collective-permute-start | bytes 1990664 | tf_op jit(solution)/shard_map/ppermute | solution.py:688
  38.6 1.1 copy-start.1
  70.6 2.4 %collective-permute-start.15 = (bf16[4,3,48,576]{3,2,1,0:T(8,128)(2,1)}, bf16[4,3,48,576]{3,2,1,0:T(8,128)(2,1)S(1)}, u32[]{:S(2)}, u32[]{:S(2)}) collective-permute-start(bf16[4,3,48,576]{3,2,1,0:T(8,128)(2,1)} %pad_maximum_fusion.1.refs_0_), channel_id=1, source_target_pairs={{0,1},{1,0},{2,3},{3,2},{4,5},{5,4},{6,7},{7,6},{8,9},{9,8},{10,11... | collective-permute-start | bytes 1990664 | tf_op jit(solution)/shard_map/ppermute | solution.py:692
  70.6 4.5 %collective-permute-start.16 = (bf16[4,3,48,576]{3,2,1,0:T(8,128)(2,1)}, bf16[4,3,48,576]{3,2,1,0:T(8,128)(2,1)S(1)}, u32[]{:S(2)}, u32[]{:S(2)}) collective-permute-start(bf16[4,3,48,576]{3,2,1,0:T(8,128)(2,1)} %collective-permute-done.9.refs_1_), channel_id=1, source_target_pairs={{0,1},{1,0},{2,3},{3,2},{4,5},{5,4},{6,7},{7,6},{8,9},{9,8},{10,11... | collective-permute-start | bytes 1990664 | tf_op jit(solution)/shard_map/ppermute | solution.py:692
  71.1 5.1 %collective-permute-start.17 = (bf16[4,3,48,576]{3,2,1,0:T(8,128)(2,1)}, bf16[4,3,48,576]{3,2,1,0:T(8,128)(2,1)S(1)}, u32[]{:S(2)}, u32[]{:S(2)}) collective-permute-start(bf16[4,3,48,576]{3,2,1,0:T(8,128)(2,1)} %collective-permute-done.10.refs_2_), channel_id=1, source_target_pairs={{0,1},{1,0},{2,3},{3,2},{4,5},{5,4},{6,7},{7,6},{8,9},{9,8},{10,11... | collective-permute-start | bytes 1990664 | tf_op jit(solution)/shard_map/ppermute | solution.py:692
  71.2 5.1 %collective-permute-start.18 = (bf16[4,3,48,576]{3,2,1,0:T(8,128)(2,1)}, bf16[4,3,48,576]{3,2,1,0:T(8,128)(2,1)}, u32[]{:S(2)}, u32[]{:S(2)}) collective-permute-start(bf16[4,3,48,576]{3,2,1,0:T(8,128)(2,1)} %collective-permute-done.11.refs_3_), channel_id=1, source_target_pairs={{0,1},{1,0},{2,3},{3,2},{4,5},{5,4},{6,7},{7,6},{8,9},{9,8},{10,11... | collective-permute-start | bytes 1990664 | tf_op jit(solution)/shard_map/ppermute | solution.py:692
  73.1 3.2 %copy-start.16 = (bf16[4,3,48,576]{3,2,1,0:T(8,128)(2,1)}, bf16[4,3,48,576]{3,2,1,0:T(8,128)(2,1)S(1)}, u32[]{:S(2)}) copy-start(bf16[4,3,48,576]{3,2,1,0:T(8,128)(2,1)S(1)} %collective-permute-done.15.refs_4_) | copy-start | bytes 1990660
  75.2 1.1 copy-start.17
  76.2 0.9 copy-start.18
  131.8 7.8 %collective-permute-start.19 = (bf16[4,3,192,576]{3,2,1,0:T(8,128)(2,1)}, bf16[4,3,192,576]{3,2,1,0:T(8,128)(2,1)}, u32[]{:S(2)}, u32[]{:S(2)}) collective-permute-start(bf16[4,3,192,576]{3,2,1,0:T(8,128)(2,1)} %get-tuple-element.112), channel_id=1, source_target_pairs={{0,1},{1,0},{2,3},{3,2},{4,5},{5,4},{6,7},{7,6},{8,9},{9,8},{10,11... | collective-permute-start | bytes 7962632 | tf_op jit(solution)/shard_map/ppermute | solution.py:692
  132.0 7.6 %copy-start = (bf16[4,3,192,576]{3,2,1,0:T(8,128)(2,1)S(1)}, bf16[4,3,192,576]{3,2,1,0:T(8,128)(2,1)}, u32[]{:S(2)}) copy-start(bf16[4,3,192,576]{3,2,1,0:T(8,128)(2,1)} %get-tuple-element.118) | copy-start | bytes 7962628
  143.3 37.4 %collective-permute-start.20 = (bf16[3,192,576]{2,1,0:T(8,128)(2,1)}, bf16[3,192,576]{2,1,0:T(8,128)(2,1)S(1)}, u32[]{:S(2)}, u32[]{:S(2)}) collective-permute-start(bf16[3,192,576]{2,1,0:T(8,128)(2,1)} %get-tuple-element.122), channel_id=1, source_target_pairs={{0,2},{2,0},{4,6},{6,4},{8,10},{10,8},{12,14},{14,12},{16,18},{18,... | collective-permute-start | bytes 1990664 | tf_op jit(solution)/shard_map/ppermute | solution.py:688
  144.1 36.6 %collective-permute-start.21 = (bf16[3,192,576]{2,1,0:T(8,128)(2,1)}, bf16[3,192,576]{2,1,0:T(8,128)(2,1)S(1)}, u32[]{:S(2)}, u32[]{:S(2)}) collective-permute-start(bf16[3,192,576]{2,1,0:T(8,128)(2,1)} %get-tuple-element.123), channel_id=1, source_target_pairs={{0,4},{2,6},{4,0},{6,2},{8,12},{10,14},{12,8},{14,10},{16,20},{18,... | collective-permute-start | bytes 1990664 | tf_op jit(solution)/shard_map/ppermute | solution.py:688
  145.4 35.3 %collective-permute-start.22 = (bf16[3,192,576]{2,1,0:T(8,128)(2,1)}, bf16[3,192,576]{2,1,0:T(8,128)(2,1)S(1)}, u32[]{:S(2)}, u32[]{:S(2)}) collective-permute-start(bf16[3,192,576]{2,1,0:T(8,128)(2,1)} %get-tuple-element.124), channel_id=1, source_target_pairs={{0,6},{2,4},{4,2},{6,0},{8,14},{10,12},{12,10},{14,8},{16,22},{18,... | collective-permute-start | bytes 1990664 | tf_op jit(solution)/shard_map/ppermute | solution.py:688
  180.7 1.2 copy-start.14
  181.1 3.5 %copy-start.2 = (bf16[4,208,576]{2,1,0:T(8,128)(2,1)S(1)}, bf16[4,208,576]{2,1,0:T(8,128)(2,1)}, u32[]{:S(2)}) copy-start(bf16[4,208,576]{2,1,0:T(8,128)(2,1)} %get-tuple-element.137) | copy-start | bytes 2875396
  181.9 2.7 %collective-permute-start.23 = (bf16[4,208,576]{2,1,0:T(8,128)(2,1)S(1)}, bf16[4,208,576]{2,1,0:T(8,128)(2,1)S(1)}, u32[]{:S(2)}, u32[]{:S(2)}) collective-permute-start(bf16[4,208,576]{2,1,0:T(8,128)(2,1)S(1)} %copy-done.14), channel_id=1, source_target_pairs={{0,1},{1,0},{2,3},{3,2},{4,5},{5,4},{6,7},{7,6},{8,9},{9,8},{10,11... | collective-permute-start | bytes 2875400 | tf_op jit(solution)/shard_map/ppermute | solution.py:692
  181.9 7.1 %collective-permute-start.27 = (bf16[3,48,576]{2,1,0:T(8,128)(2,1)S(1)}, bf16[3,48,576]{2,1,0:T(8,128)(2,1)S(1)}, u32[]{:S(2)}, u32[]{:S(2)}) collective-permute-start(bf16[3,48,576]{2,1,0:T(8,128)(2,1)S(1)} %get-tuple-element.150), channel_id=1, source_target_pairs={{0,8},{2,10},{4,12},{6,14},{8,0},{10,2},{12,4},{14,6},{16,24},{18,... | collective-permute-start | bytes 497672 | tf_op jit(solution)/shard_map/ppermute | solution.py:688
  184.9 18.4 %collective-permute-start.24 = (bf16[208,576]{1,0:T(8,128)(2,1)S(1)}, bf16[208,576]{1,0:T(8,128)(2,1)S(1)}, u32[]{:S(2)}, u32[]{:S(2)}) collective-permute-start(bf16[208,576]{1,0:T(8,128)(2,1)S(1)} %get-tuple-element.146), channel_id=1, source_target_pairs={{0,2},{2,0},{4,6},{6,4},{8,10},{10,8},{12,14},{14,12},{16,18},{18,... | collective-permute-start | bytes 718856 | tf_op jit(solution)/shard_map/ppermute | solution.py:688
  185.7 17.5 %collective-permute-start.25 = (bf16[208,576]{1,0:T(8,128)(2,1)S(1)}, bf16[208,576]{1,0:T(8,128)(2,1)S(1)}, u32[]{:S(2)}, u32[]{:S(2)}) collective-permute-start(bf16[208,576]{1,0:T(8,128)(2,1)S(1)} %get-tuple-element.147), channel_id=1, source_target_pairs={{0,4},{2,6},{4,0},{6,2},{8,12},{10,14},{12,8},{14,10},{16,20},{18,... | collective-permute-start | bytes 718856 | tf_op jit(solution)/shard_map/ppermute | solution.py:688
  187.0 16.2 %collective-permute-start.26 = (bf16[208,576]{1,0:T(8,128)(2,1)S(1)}, bf16[208,576]{1,0:T(8,128)(2,1)S(1)}, u32[]{:S(2)}, u32[]{:S(2)}) collective-permute-start(bf16[208,576]{1,0:T(8,128)(2,1)S(1)} %get-tuple-element.148), channel_id=1, source_target_pairs={{0,6},{2,4},{4,2},{6,0},{8,14},{10,12},{12,10},{14,8},{16,22},{18,... | collective-permute-start | bytes 718856 | tf_op jit(solution)/shard_map/ppermute | solution.py:688
  188.4 14.8 %collective-permute-start.28 = (bf16[3,48,576]{2,1,0:T(8,128)(2,1)S(1)}, bf16[3,48,576]{2,1,0:T(8,128)(2,1)S(1)}, u32[]{:S(2)}, u32[]{:S(2)}) collective-permute-start(bf16[3,48,576]{2,1,0:T(8,128)(2,1)S(1)} %get-tuple-element.151), channel_id=1, source_target_pairs={{0,16},{2,18},{4,20},{6,22},{8,24},{10,26},{12,28},{14,30},{16,0},... | collective-permute-start | bytes 497672 | tf_op jit(solution)/shard_map/ppermute | solution.py:688
  189.0 13.0 %copy-start.5 = (bf16[3,48,576]{2,1,0:T(8,128)(2,1)}, bf16[3,48,576]{2,1,0:T(8,128)(2,1)S(1)}, u32[]{:S(2)}) copy-start(bf16[3,48,576]{2,1,0:T(8,128)(2,1)S(1)} %collective-permute-done.27.refs_5_) | copy-start | bytes 497668
  189.0 14.2 %collective-permute-start.29 = (bf16[3,48,576]{2,1,0:T(8,128)(2,1)S(1)}, bf16[3,48,576]{2,1,0:T(8,128)(2,1)S(1)}, u32[]{:S(2)}, u32[]{:S(2)}) collective-permute-start(bf16[3,48,576]{2,1,0:T(8,128)(2,1)S(1)} %get-tuple-element.152), channel_id=1, source_target_pairs={{0,24},{2,26},{4,28},{6,30},{8,16},{10,18},{12,20},{14,22},{16,8},... | collective-permute-start | bytes 497672 | tf_op jit(solution)/shard_map/ppermute | solution.py:688
  203.2 14.6 %copy-start.6 = (bf16[3,48,576]{2,1,0:T(8,128)(2,1)}, bf16[3,48,576]{2,1,0:T(8,128)(2,1)S(1)}, u32[]{:S(2)}) copy-start(bf16[3,48,576]{2,1,0:T(8,128)(2,1)S(1)} %collective-permute-done.28.refs_6_) | copy-start | bytes 497668
  203.2 20.9 %collective-permute-start.34 = (bf16[2,576,512]{2,1,0:T(8,128)(2,1)}, bf16[2,576,512]{2,1,0:T(8,128)(2,1)S(1)}, u32[]{:S(2)}, u32[]{:S(2)}) collective-permute-start(bf16[2,576,512]{2,1,0:T(8,128)(2,1)} %get-tuple-element.166), channel_id=1, source_target_pairs={{0,1},{1,0},{2,3},{3,2},{4,5},{5,4},{6,7},{7,6},{8,9},{9,8},{10,11... | collective-permute-start | bytes 3538952 | tf_op jit(solution)/shard_map/ppermute | solution.py:692
  203.2 0.7 copy-start.7
  204.0 20.2 %collective-permute-start.33 = (bf16[2,576,512]{2,1,0:T(8,128)(2,1)}, bf16[2,576,512]{2,1,0:T(8,128)(2,1)S(1)}, u32[]{:S(2)}, u32[]{:S(2)}) collective-permute-start(bf16[2,576,512]{2,1,0:T(8,128)(2,1)} %get-tuple-element.165), channel_id=1, source_target_pairs={{0,1},{1,0},{2,3},{3,2},{4,5},{5,4},{6,7},{7,6},{8,9},{9,8},{10,11... | collective-permute-start | bytes 3538952 | tf_op jit(solution)/shard_map/ppermute | solution.py:692
  205.3 7.1 %collective-permute-start.31 = (bf16[64,576]{1,0:T(8,128)(2,1)S(1)}, bf16[64,576]{1,0:T(8,128)(2,1)S(1)}, u32[]{:S(2)}, u32[]{:S(2)}) collective-permute-start(bf16[64,576]{1,0:T(8,128)(2,1)S(1)} %get-tuple-element.203), channel_id=1, source_target_pairs={{0,16},{2,18},{4,20},{6,22},{8,24},{10,26},{12,28},{14,30},{16,0},... | collective-permute-start | bytes 221192 | tf_op jit(solution)/shard_map/ppermute | solution.py:688
  209.3 4.9 %collective-permute-start.30 = (bf16[64,576]{1,0:T(8,128)(2,1)S(1)}, bf16[64,576]{1,0:T(8,128)(2,1)S(1)}, u32[]{:S(2)}, u32[]{:S(2)}) collective-permute-start(bf16[64,576]{1,0:T(8,128)(2,1)S(1)} %get-tuple-element.204), channel_id=1, source_target_pairs={{0,8},{2,10},{4,12},{6,14},{8,0},{10,2},{12,4},{14,6},{16,24},{18,... | collective-permute-start | bytes 221192 | tf_op jit(solution)/shard_map/ppermute | solution.py:688
  209.3 8.6 %collective-permute-start.32 = (bf16[64,576]{1,0:T(8,128)(2,1)S(1)}, bf16[64,576]{1,0:T(8,128)(2,1)S(1)}, u32[]{:S(2)}, u32[]{:S(2)}) collective-permute-start(bf16[64,576]{1,0:T(8,128)(2,1)S(1)} %concatenate.20), channel_id=1, source_target_pairs={{0,24},{2,26},{4,28},{6,30},{8,16},{10,18},{12,20},{14,22},{16,8},... | collective-permute-start | bytes 221192 | tf_op jit(solution)/shard_map/ppermute | solution.py:688
  212.4 5.5 %copy-start.8 = (bf16[64,576]{1,0:T(8,128)(2,1)}, bf16[64,576]{1,0:T(8,128)(2,1)S(1)}, u32[]{:S(2)}) copy-start(bf16[64,576]{1,0:T(8,128)(2,1)S(1)} %collective-permute-done.31.refs_2_) | copy-start | bytes 221188
  214.1 3.7 %copy-start.9 = (bf16[64,576]{1,0:T(8,128)(2,1)}, bf16[64,576]{1,0:T(8,128)(2,1)S(1)}, u32[]{:S(2)}) copy-start(bf16[64,576]{1,0:T(8,128)(2,1)S(1)} %collective-permute-done.30.refs_1_) | copy-start | bytes 221188
  217.9 0.6 copy-start.10
  220.8 10.4 %all-to-all-start = ((f32[32,1,128]{2,1,0:T(1,128)}), f32[32,1,128]{2,1,0:T(1,128)S(1)}, u32[]{:S(2)}, u32[]{:S(2)}) async-start(f32[32,1,128]{2,1,0:T(1,128)} %get-tuple-element.170), calls=%async_computation | async-start | bytes 32768 | tf_op jit(solution)/shard_map/all_to_all | solution.py:942
  231.3 0.6 copy-start.11
